TPU v7x, 32 devices: a whole 2x2x4 slice. The times are simulated.
32 devices in a mesh: groups: 2 (over y), tm: 4 (over z), segment: 2 (over x), head: 2 (over core).
Axes of the slice: x: 2, y: 2, z: 4, core: 2. Of those that a mesh axis runs over, the one named last changes fastest.
Arguments:
- hidden_in: bfloat16 [768, 3072], P(('groups', 'tm'), 'head'), parts along dimension 0, may hold values from -6 to 6
- key_cache: bfloat16 [2, 768, 3072], P('segment', ('groups', 'tm'), 'head'), parts along dimension 1, may hold values from -6 to 6
- value_cache: bfloat16 [2, 768, 3072], P('segment', ('groups', 'tm'), 'head'), parts along dimension 1, may hold values from -6 to 6
- query_gain: float32 [2, 128], P('segment'), may hold values from 0.4 to 1.6
- key_gain: float32 [2, 128], P('segment'), may hold values from 0.4 to 1.6
- out_gate: float32 [2, 3072], P('segment', 'head'), may hold values from 0.5 to 2
- span_ids: int32 [768], P('groups'), parts along dimension 0, may hold values from 0 to 2, as said below
Outputs:
- layer_outputs: bfloat16 [2, 768, 3072], P('segment', ('groups', 'tm'), 'head'), parts along dimension 1
There are 2 independent parts, one for each index of `groups`. A program takes and returns all parts, laid end to end along the dimension named above; an argument that names none is the same for every part. Nothing has to cross between parts.
Inputs may be any that keep to these rules, and one draw needn't show every extreme that they name: span_ids never fall and rise by one from span to span; every span but the first and the last holds exactly 192 tokens, and the first and the last together hold 192, each at least one.
All inputs are finite; a program needn't handle non-finite values.
Results may differ from a plain program's by a relative error of at most 0.011.
Values may be sent and summed in bfloat16 or wider, within the bound.
No kernel may reach another device: no remote copies, remote signals or barrier semaphores. Data moves between devices by JAX's collectives and lax.ppermute only.
A program may use at most 64 MiB of HBM per device.

v0:
```python
import functools
import math

import jax
import jax.numpy as jnp
from jax import lax
from jax.experimental import pallas as pl
from jax.experimental.pallas import tpu as pltpu
from jax.sharding import PartitionSpec as P


HEAD_DIM = 128
PART_ROWS = 16
BLOCKED = -1e30
PACK_GRANT = 54880 << 10


def passed_along(shard, axis, by):
    devices = lax.axis_size(axis)
    pairs = [(i, i + by) for i in range(devices) if 0 <= i + by < devices]
    return lax.ppermute(shard, axis, pairs)


def head_normalize(features, gain_row):
    row_count = features.shape[0]
    shaped = features.astype(jnp.float32).reshape(row_count, -1, HEAD_DIM)
    inverse_rms = lax.rsqrt(jnp.mean(shaped * shaped, axis=-1, keepdims=True) + 1e-06)
    return (shaped * inverse_rms * gain_row).reshape(features.shape).astype(jnp.bfloat16)


def attend_heads(queries, key_rows, value_rows, query_ids, key_ids):
    row_count = queries.shape[0]
    key_count = key_rows.shape[0]
    pair_width = 2 * HEAD_DIM
    group_count = queries.shape[1] // pair_width
    score_scale = 2.0 / math.sqrt(HEAD_DIM)
    allowed = (key_ids[None, :] <= query_ids[:, None]) & (
        key_ids[None, :] >= query_ids[:, None] - 2
    )

    def pair_step(group_index, result):
        column = group_index * pair_width
        query_pair = lax.dynamic_slice_in_dim(queries, column, pair_width, 1).reshape(
            row_count, 2, HEAD_DIM
        )
        key_pair = lax.dynamic_slice_in_dim(key_rows, column, pair_width, 1).reshape(
            key_count, 2, HEAD_DIM
        )
        value_pair = lax.dynamic_slice_in_dim(value_rows, column, pair_width, 1).reshape(
            key_count, 2, HEAD_DIM
        )
        scores = (
            jnp.einsum("rhd,khd->hrk", query_pair, key_pair, preferred_element_type=jnp.float32)
            * score_scale
        )
        weights = jnp.where(allowed[None], jnp.exp(scores), 0.0)
        denominator = jnp.sum(weights, axis=-1)
        mixture = jnp.einsum(
            "hrk,khd->rhd",
            weights.astype(jnp.bfloat16),
            value_pair,
            preferred_element_type=jnp.float32,
        )
        mixture = mixture / jnp.transpose(denominator)[:, :, None]
        return lax.dynamic_update_slice_in_dim(
            result, mixture.reshape(row_count, pair_width), column, 1
        )

    initial = jnp.zeros((row_count, queries.shape[1]), jnp.float32)
    return lax.fori_loop(0, group_count, pair_step, initial)


def body(hidden_in, key_cache, value_cache, query_gain, key_gain, out_gate, span_ids):
    block_rows = hidden_in.shape[0]
    tm_index = lax.axis_index("tm")
    segment_index = lax.axis_index("segment")
    normed_keys = head_normalize(key_cache[0], key_gain[0])
    own_values = value_cache[0]
    first_row = tm_index * block_rows
    all_keys, all_values = (
        lax.all_gather(normed_keys, "tm", axis=0, tiled=True),
        lax.all_gather(own_values, "tm", axis=0, tiled=True),
    )

    def update(row_block):
        queries = head_normalize(row_block, query_gain[0])
        query_ids = lax.dynamic_slice_in_dim(span_ids, first_row, row_block.shape[0], 0)
        mixture = attend_heads(queries, all_keys, all_values, query_ids, span_ids)
        return (row_block.astype(jnp.float32) + out_gate[0] * mixture).astype(jnp.bfloat16)

    segments = lax.axis_size("segment")
    current = hidden_in
    result = hidden_in
    for section in range(segments):
        active = segment_index == section
        produced = lax.cond(active, lambda inputs: update(inputs), lambda inputs: inputs, current)
        result = jnp.where(active, produced, result)
        if section + 1 < segments:
            arrived = passed_along(produced, "segment", 1)
            current = jnp.where(segment_index == section + 1, arrived, current)
    return result[None]


MESH_TAIL = ("tm", "segment", "head")


def swapped(array, offset, blocks):
    at = lambda t, s, c: (t * 2 + s) * 2 + c
    pairs = [
        (at(t, s, c), at(t ^ offset, c, s))
        for t in range(blocks)
        for s in range(2)
        for c in range(2)
    ]
    return lax.ppermute(array, MESH_TAIL, pairs)


def normed(rows, gain):
    rows = rows.astype(jnp.float32)
    inverse_rms = lax.rsqrt(jnp.mean(rows * rows, axis=-1, keepdims=True) + 1e-06)
    return (rows * inverse_rms * gain).astype(jnp.bfloat16)


def split_parts(row):
    high = row.astype(jnp.bfloat16)
    rest = row - high.astype(jnp.float32)
    middle = rest.astype(jnp.bfloat16)
    low = (rest - middle.astype(jnp.float32)).astype(jnp.bfloat16)
    return [part.astype(jnp.float32) for part in (high, middle, low)]


def pack_kernel(offset, key_hbm, value_hbm, hidden_hbm, qgain_hbm, kgain_hbm, gate_hbm, *refs):
    out, kgain, qgain, gate, sems = refs[-5:]
    rows = key_hbm.shape[0]
    width = out.shape[1]
    half = rows // 2
    tm = lax.axis_index("tm")
    first = pl.multiple_of(lax.axis_index("segment") * half, 16)
    columns = pl.ds(pl.multiple_of((tm ^ offset) * width, 128), width)
    moves = [
        (key_hbm.at[:, columns], out.at[pl.ds(0, rows)]),
        (kgain_hbm, kgain),
        (value_hbm.at[:, columns], out.at[pl.ds(rows, rows)]),
        (hidden_hbm.at[pl.ds(first, half), columns], out.at[pl.ds(2 * rows, half)]),
    ]
    if offset == 0:
        moves += [(qgain_hbm, qgain), (gate_hbm.at[:, columns], gate)]
    copies = []
    for which, (source, target) in enumerate(moves):
        copy = pltpu.make_async_copy(source, target, sems.at[which])
        copy.start()
        copies.append(copy)
    copies[0].wait()
    copies[1].wait()
    gain = kgain[...]
    for head in range(width // HEAD_DIM):
        lanes = pl.ds(head * HEAD_DIM, HEAD_DIM)
        out[pl.ds(0, rows), lanes] = normed(out[pl.ds(0, rows), lanes], gain)
    for copy in copies[2:]:
        copy.wait()
    if offset == 0:
        query_row = jnp.concatenate([qgain[...]] * (width // HEAD_DIM), axis=1)
        parts = split_parts(gate[...]) + split_parts(query_row)
        index = lax.broadcasted_iota(jnp.int32, (PART_ROWS, width), 0)
        table = jnp.zeros((PART_ROWS, width), jnp.float32)
        for line, part in enumerate(parts):
            table = jnp.where(index == line, part, table)
        out[pl.ds(2 * rows + half, PART_ROWS), :] = table.astype(jnp.bfloat16)


def layer_rows(current, keys, values, bias, query_gain, gate):
    scale = 2.0 / math.sqrt(HEAD_DIM) * math.log2(math.e)
    queries = normed(current, query_gain)
    scores = lax.dot_general(
        queries, keys, (((1,), (1,)), ((), ())), preferred_element_type=jnp.float32
    )
    weights = jnp.exp2(scores * scale + bias)
    denominator = jnp.sum(weights, axis=-1, keepdims=True)
    mixture = jnp.dot(weights.astype(jnp.bfloat16), values, preferred_element_type=jnp.float32)
    mixture = mixture / denominator
    return (current.astype(jnp.float32) + gate * mixture).astype(jnp.bfloat16)


def attend_kernel(offsets, rows, key_ids, query_ids, *refs):
    count = len(offsets)
    own, other, outs = refs[:count], refs[count : 2 * count], refs[2 * count : 3 * count]
    bias_ref = refs[3 * count]
    width = outs[0].shape[1]
    half = rows // 2
    core = lax.axis_index("head")
    keys_row, queries_column = key_ids[...], query_ids[...]
    allowed = (keys_row <= queries_column) & (keys_row >= queries_column - 2)
    bias_ref[...] = jnp.where(allowed, 0.0, BLOCKED)

    def run(first, second, last):
        for head in range(width // HEAD_DIM):
            lanes = pl.ds(head * HEAD_DIM, HEAD_DIM)
            bias = bias_ref[...]

            def part(refs_, start, size):
                return jnp.concatenate([ref[pl.ds(start, size), lanes] for ref in refs_], axis=0)

            def table(refs_, line):
                at = offsets.index(0)
                block = refs_[at][pl.ds(2 * rows + half, PART_ROWS), lanes].astype(jnp.float32)
                return block[line : line + 1] + (
                    block[line + 1 : line + 2] + block[line + 2 : line + 3]
                )

            current = jnp.concatenate(
                [ref[pl.ds(2 * rows, half), lanes] for at in range(count) for ref in (first[at], second[at])],
                axis=0,
            )
            for section in range(last + 1):
                source = (first, second)[section]
                current = layer_rows(
                    current,
                    part(source, 0, rows),
                    part(source, rows, rows),
                    bias,
                    table(source, 3),
                    table(source, 0),
                )
            for at in range(count):
                outs[at][:, lanes] = current[at * rows : (at + 1) * rows]

    @pl.when(core == 0)
    def _():
        run(own, other, 0)

    @pl.when(core != 0)
    def _():
        run(other, own, 1)


def join_kernel(offsets, *refs):
    out = refs[len(offsets)]
    width = refs[0].shape[1]
    tm = lax.axis_index("tm")
    for at, offset in enumerate(offsets):
        out[:, pl.ds(pl.multiple_of((tm ^ offset) * width, 128), width)] = refs[at][...]


def grant(size):
    return pltpu.CompilerParams(vmem_limit_bytes=size)


def by_heads(hidden_in, key_cache, value_cache, query_gain, key_gain, out_gate, span_ids):
    rows, features = hidden_in.shape
    blocks = lax.axis_size("tm")
    width = features // blocks
    half = rows // 2
    total = rows * blocks
    tm = lax.axis_index("tm")
    offsets = send_order(blocks)
    vmem = pl.BlockSpec(memory_space=pltpu.VMEM)
    hbm = pl.BlockSpec(memory_space=pltpu.HBM)
    anywhere = pl.BlockSpec(memory_space=pl.ANY)

    ids = jnp.concatenate(
        [lax.dynamic_slice_in_dim(span_ids, (tm ^ offset) * rows, rows, 0) for offset in offsets]
    )
    ids_row, ids_column = ids.reshape(1, total), ids.reshape(total, 1)

    def pack(at, *after):
        offset = offsets[at]
        size = 2 * rows + half + (PART_ROWS if offset == 0 else 0)
        payload = pl.pallas_call(
            functools.partial(pack_kernel, offset),
            out_shape=jax.ShapeDtypeStruct((size, width), jnp.bfloat16),
            in_specs=[hbm] * 6 + [anywhere] * len(after),
            out_specs=vmem,
            scratch_shapes=[
                pltpu.VMEM((1, HEAD_DIM), jnp.float32),
                pltpu.VMEM((1, HEAD_DIM), jnp.float32),
                pltpu.VMEM((1, width), jnp.float32),
                pltpu.SemaphoreType.DMA((6,)),
            ],
            compiler_params=grant(PACK_GRANT),
        )(key_cache[0], value_cache[0], hidden_in, query_gain, key_gain, out_gate, *after)
        return payload

    own, other = [], []
    for at, offset in enumerate(offsets):
        payload = pack(at, *((ids_row, ids_column) if at == blocks - 1 else ()))
        own.append(swapped(payload, offset, blocks))
    for payload in own:
        other.append(lax.ppermute(payload, "head", [(0, 1), (1, 0)]))
    results = pl.pallas_call(
        functools.partial(attend_kernel, offsets, rows),
        out_shape=[jax.ShapeDtypeStruct((rows, width), jnp.bfloat16)] * blocks,
        in_specs=[vmem] * (2 + 2 * blocks),
        out_specs=[vmem] * blocks,
        scratch_shapes=[pltpu.VMEM((total, total), jnp.float32)],
        compiler_params=grant(12 << 20),
        name="attend",
    )(ids_row, ids_column, *own, *other)
    back = []
    for at, offset in enumerate(offsets):
        back.append(swapped(results[at], offset, blocks))
    joined = pl.pallas_call(
        functools.partial(join_kernel, offsets),
        out_shape=jax.ShapeDtypeStruct((rows, features), jnp.bfloat16),
        in_specs=[vmem] * blocks,
        out_specs=vmem,
        compiler_params=grant(2 << 20),
        name="join",
    )(*back)
    return joined[None]


def send_order(blocks):
    far = blocks // 2
    return tuple(range(far, blocks)) + tuple(reversed(range(far)))


def solution(mesh):
    placed = (
        P(("groups", "tm"), "head"),
        P("segment", ("groups", "tm"), "head"),
        P("segment", ("groups", "tm"), "head"),
        P("segment", None),
        P("segment", None),
        P("segment", "head"),
        P("groups"),
    )
    blocks = mesh.shape["tm"]
    two_by_two = mesh.shape["segment"] == 2 and mesh.shape["head"] == 2
    mapped = functools.partial(
        jax.shard_map,
        mesh=mesh,
        in_specs=placed,
        out_specs=P("segment", ("groups", "tm"), "head"),
        check_vma=False,
    )

    def run(hidden_in, *rest):
        rows = hidden_in.shape[0] // (mesh.shape["groups"] * blocks)
        features = hidden_in.shape[1] // mesh.shape["head"]
        fits = features % (blocks * HEAD_DIM) == 0 and rows % 32 == 0
        if two_by_two and blocks & (blocks - 1) == 0 and fits:
            step = mapped(by_heads)
        else:
            step = mapped(body)
        return step(hidden_in, *rest)

    return run
```

profile of v0, /device:TPU:1, one launch (start us, length us, event | category | flops | bytes accessed | tf_op | source)
XLA Modules:
  0.0 42.3 jit_solution(14285586100215398197)
XLA Ops:
  0.0 0.7 %copy-done.4 = s32[384]{0:T(512)S(1)} copy-done((s32[384]{0:T(512)S(1)}, s32[384]{0:T(512)}, u32[]{:S(2)}) %copy-start.4) | copy-done | bytes 1560
  0.9 0.8 %reshape.8.refs_1_.query_ids = s32[384,1]{1,0:T(8,128)} reshape(s32[384]{0:T(512)S(1)} %pad_add_fusion) | data formatting | bytes 3072 | tf_op jit(solution)/shard_map/reshape | solution.py:263
  1.7 0.6 %copy-done.2 = f32[1,128]{1,0:T(1,128)S(1)} copy-done((f32[1,128]{1,0:T(1,128)S(1)}, f32[1,128]{1,0:T(1,128)}, u32[]{:S(2)}) %copy-start.2) | copy-done | bytes 536
  2.3 1.1 %shard_map.76 = bf16[256,384]{1,0:T(8,128)(2,1)S(1)} custom-call(bf16[96,1536]{1,0:T(8,128)(2,1)} %bitcast.3, bf16[96,1536]{1,0:T(8,128)(2,1)} %bitcast.7, bf16[96,1536]{1,0:T(8,128)(2,1)} %hidden_hbm.7, f32[1,128]{1,0:T(1,128)S(1)} %copy-done.2, f32[1,128]{1,0:T(1,128)S(1)} %copy-done.3, f32[1,1536]{1,0:T(1,128)S(1)} %copy-done.1, ...), custom_call_target="tpu_custom_call" | custom-call | tf_op jit(solution)/shard_map/pallas_call | solution.py:268
  3.4 4.5 %collective-permute-start.3 = (bf16[256,384]{1,0:T(8,128)(2,1)S(1)}, bf16[256,384]{1,0:T(8,128)(2,1)S(1)}, u32[]{:S(2)}, u32[]{:S(2)}) collective-permute-start(bf16[256,384]{1,0:T(8,128)(2,1)S(1)} %shard_map.76), channel_id=1, source_target_pairs={{0,0},{1,2},{2,1},{3,3},{4,4},{5,6},{6,5},{7,7},{8,8},{9,10},{10,9... | collective-permute-start | bytes 589832 | tf_op jit(solution)/shard_map/ppermute | solution.py:115
  7.9 1.1 %shard_map.73 = bf16[240,384]{1,0:T(8,128)(2,1)S(1)} custom-call(bf16[96,1536]{1,0:T(8,128)(2,1)} %bitcast.4, bf16[96,1536]{1,0:T(8,128)(2,1)} %bitcast.8, bf16[96,1536]{1,0:T(8,128)(2,1)} %hidden_hbm.7, f32[1,128]{1,0:T(1,128)S(1)} %copy-done.2, f32[1,128]{1,0:T(1,128)S(1)} %copy-done.3, f32[1,1536]{1,0:T(1,128)S(1)} %copy-done.1), custom_call_target="tpu_custom_call" | custom-call | tf_op jit(solution)/shard_map/pallas_call | solution.py:268
  9.0 2.1 %collective-permute-start = (bf16[240,384]{1,0:T(8,128)(2,1)S(1)}, bf16[240,384]{1,0:T(8,128)(2,1)S(1)}, u32[]{:S(2)}, u32[]{:S(2)}) collective-permute-start(bf16[240,384]{1,0:T(8,128)(2,1)S(1)} %shard_map.73), channel_id=1, source_target_pairs={{0,8},{1,10},{2,9},{3,11},{4,12},{5,14},{6,13},{7,15},{8,0},{9,2},... | collective-permute-start | bytes 552968 | tf_op jit(solution)/shard_map/ppermute | solution.py:115
  11.1 1.1 %shard_map.74 = bf16[240,384]{1,0:T(8,128)(2,1)S(1)} custom-call(bf16[96,1536]{1,0:T(8,128)(2,1)} %bitcast.5, bf16[96,1536]{1,0:T(8,128)(2,1)} %bitcast.9, bf16[96,1536]{1,0:T(8,128)(2,1)} %hidden_hbm.7, f32[1,128]{1,0:T(1,128)S(1)} %copy-done.2, f32[1,128]{1,0:T(1,128)S(1)} %copy-done.3, f32[1,1536]{1,0:T(1,128)S(1)} %copy-done.1), custom_call_target="tpu_custom_call" | custom-call | tf_op jit(solution)/shard_map/pallas_call | solution.py:268
  12.2 2.6 %collective-permute-start.1 = (bf16[240,384]{1,0:T(8,128)(2,1)S(1)}, bf16[240,384]{1,0:T(8,128)(2,1)S(1)}, u32[]{:S(2)}, u32[]{:S(2)}) collective-permute-start(bf16[240,384]{1,0:T(8,128)(2,1)S(1)} %shard_map.74), channel_id=1, source_target_pairs={{0,12},{1,14},{2,13},{3,15},{4,8},{5,10},{6,9},{7,11},{8,4},{9,6},... | collective-permute-start | bytes 552968 | tf_op jit(solution)/shard_map/ppermute | solution.py:115
  14.8 1.1 %shard_map.75 = bf16[240,384]{1,0:T(8,128)(2,1)S(1)} custom-call(bf16[96,1536]{1,0:T(8,128)(2,1)} %bitcast.6, bf16[96,1536]{1,0:T(8,128)(2,1)} %bitcast.10, bf16[96,1536]{1,0:T(8,128)(2,1)} %hidden_hbm.7, f32[1,128]{1,0:T(1,128)S(1)} %copy-done.2, f32[1,128]{1,0:T(1,128)S(1)} %copy-done.3, f32[1,1536]{1,0:T(1,128)S(1)} %copy-done.1), custom_call_target="tpu_custom_call" | custom-call | tf_op jit(solution)/shard_map/pallas_call | solution.py:268
  15.9 0.3 collective-permute-start.2
  16.2 7.5 %collective-permute-done.refs_0_ = bf16[240,384]{1,0:T(8,128)(2,1)S(1)} collective-permute-done((bf16[240,384]{1,0:T(8,128)(2,1)S(1)}, bf16[240,384]{1,0:T(8,128)(2,1)S(1)}, u32[]{:S(2)}, u32[]{:S(2)}) %collective-permute-start) | collective-permute-done | bytes 184352 | tf_op jit(solution)/shard_map/ppermute | solution.py:115
  23.7 0.5 %collective-permute-start.5 = (bf16[240,384]{1,0:T(8,128)(2,1)S(1)}, bf16[240,384]{1,0:T(8,128)(2,1)S(1)}, u32[]{:S(2)}, u32[]{:S(2)}) collective-permute-start(bf16[240,384]{1,0:T(8,128)(2,1)S(1)} %collective-permute-done.1.refs_1_), channel_id=1, source_target_pairs={{0,1},{1,0},{2,3},{3,2},{4,5},{5,4},{6,7},{7,6},{8,9},{9,8},{10,11... | collective-permute-start | bytes 552968 | tf_op jit(solution)/shard_map/ppermute | solution.py:288
  24.5 2.0 %collective-permute-start.6 = (bf16[240,384]{1,0:T(8,128)(2,1)S(1)}, bf16[240,384]{1,0:T(8,128)(2,1)S(1)}, u32[]{:S(2)}, u32[]{:S(2)}) collective-permute-start(bf16[240,384]{1,0:T(8,128)(2,1)S(1)} %collective-permute-done.2.refs_2_), channel_id=1, source_target_pairs={{0,1},{1,0},{2,3},{3,2},{4,5},{5,4},{6,7},{7,6},{8,9},{9,8},{10,11... | collective-permute-start | bytes 552968 | tf_op jit(solution)/shard_map/ppermute | solution.py:288
  26.5 1.0 %collective-permute-done.6.refs_6_ = bf16[240,384]{1,0:T(8,128)(2,1)S(1)} collective-permute-done((bf16[240,384]{1,0:T(8,128)(2,1)S(1)}, bf16[240,384]{1,0:T(8,128)(2,1)S(1)}, u32[]{:S(2)}, u32[]{:S(2)}) %collective-permute-start.6) | collective-permute-done | bytes 184352 | tf_op jit(solution)/shard_map/ppermute | solution.py:288
  27.5 2.4 %attend.1 = (bf16[96,384]{1,0:T(8,128)(2,1)S(1)}, bf16[96,384]{1,0:T(8,128)(2,1)S(1)}, bf16[96,384]{1,0:T(8,128)(2,1)S(1)}, bf16[96,384]{1,0:T(8,128)(2,1)S(1)}) custom-call(s32[1,384]{1,0:T(1,128)S(1)} %reshape.6.refs_0_.key_ids, s32[384,1]{1,0:T(8,128)S(1)} %copy-done, bf16[240,384]{1,0:T(8,128)(2,1)S(1)} %collective-permute-done.refs_0_, ...), custom_call_target="tpu_custom_call" | custom-call | tf_op jit(solution)/shard_map/attend/pallas_call | solution.py:289
  29.9 3.1 %collective-permute-start.8 = (bf16[96,384]{1,0:T(8,128)(2,1)S(1)}, bf16[96,384]{1,0:T(8,128)(2,1)S(1)}, u32[]{:S(2)}, u32[]{:S(2)}) collective-permute-start(bf16[96,384]{1,0:T(8,128)(2,1)S(1)} %get-tuple-element.9), channel_id=1, source_target_pairs={{0,8},{1,10},{2,9},{3,11},{4,12},{5,14},{6,13},{7,15},{8,0},{9,2},... | collective-permute-start | bytes 221192 | tf_op jit(solution)/shard_map/ppermute | solution.py:115
  33.0 1.5 %collective-permute-start.9 = (bf16[96,384]{1,0:T(8,128)(2,1)S(1)}, bf16[96,384]{1,0:T(8,128)(2,1)S(1)}, u32[]{:S(2)}, u32[]{:S(2)}) collective-permute-start(bf16[96,384]{1,0:T(8,128)(2,1)S(1)} %get-tuple-element.10), channel_id=1, source_target_pairs={{0,12},{1,14},{2,13},{3,15},{4,8},{5,10},{6,9},{7,11},{8,4},{9,6},... | collective-permute-start | bytes 221192 | tf_op jit(solution)/shard_map/ppermute | solution.py:115
  34.7 2.5 %collective-permute-start.11 = (bf16[96,384]{1,0:T(8,128)(2,1)S(1)}, bf16[96,384]{1,0:T(8,128)(2,1)S(1)}, u32[]{:S(2)}, u32[]{:S(2)}) collective-permute-start(bf16[96,384]{1,0:T(8,128)(2,1)S(1)} %get-tuple-element.12), channel_id=1, source_target_pairs={{0,0},{1,2},{2,1},{3,3},{4,4},{5,6},{6,5},{7,7},{8,8},{9,10},{10,9... | collective-permute-start | bytes 221192 | tf_op jit(solution)/shard_map/ppermute | solution.py:115
  37.2 0.7 %collective-permute-done.8.refs_0_ = bf16[96,384]{1,0:T(8,128)(2,1)S(1)} collective-permute-done((bf16[96,384]{1,0:T(8,128)(2,1)S(1)}, bf16[96,384]{1,0:T(8,128)(2,1)S(1)}, u32[]{:S(2)}, u32[]{:S(2)}) %collective-permute-start.8) | collective-permute-done | bytes 73760 | tf_op jit(solution)/shard_map/ppermute | solution.py:115
  37.9 2.4 %collective-permute-done.9.refs_1_ = bf16[96,384]{1,0:T(8,128)(2,1)S(1)} collective-permute-done((bf16[96,384]{1,0:T(8,128)(2,1)S(1)}, bf16[96,384]{1,0:T(8,128)(2,1)S(1)}, u32[]{:S(2)}, u32[]{:S(2)}) %collective-permute-start.9) | collective-permute-done | bytes 73760 | tf_op jit(solution)/shard_map/ppermute | solution.py:115
  40.3 0.7 %collective-permute-done.10.refs_2_ = bf16[96,384]{1,0:T(8,128)(2,1)S(1)} collective-permute-done((bf16[96,384]{1,0:T(8,128)(2,1)S(1)}, bf16[96,384]{1,0:T(8,128)(2,1)S(1)}, u32[]{:S(2)}, u32[]{:S(2)}) %collective-permute-start.10) | collective-permute-done | bytes 73760 | tf_op jit(solution)/shard_map/ppermute | solution.py:115
  41.0 0.5 %collective-permute-done.11.refs_3_ = bf16[96,384]{1,0:T(8,128)(2,1)S(1)} collective-permute-done((bf16[96,384]{1,0:T(8,128)(2,1)S(1)}, bf16[96,384]{1,0:T(8,128)(2,1)S(1)}, u32[]{:S(2)}, u32[]{:S(2)}) %collective-permute-start.11) | collective-permute-done | bytes 73760 | tf_op jit(solution)/shard_map/ppermute | solution.py:115
  41.6 0.8 %join.1 = bf16[96,1536]{1,0:T(8,128)(2,1)} custom-call(bf16[96,384]{1,0:T(8,128)(2,1)S(1)} %collective-permute-done.8.refs_0_, bf16[96,384]{1,0:T(8,128)(2,1)S(1)} %collective-permute-done.9.refs_1_, bf16[96,384]{1,0:T(8,128)(2,1)S(1)} %collective-permute-done.10.refs_2_, bf16[96,384]{1,0:T(8,128)(2,1)S(1)} %collective-permute-done.11.refs_3_), custom_call_target="tpu_custom_call" | custom-call | tf_op jit(solution)/shard_map/join/pallas_call | solution.py:301
  (20 shorter events, 0.6 us)
Async XLA Ops:
  0.0 0.7 %copy-start.4 = (s32[384]{0:T(512)S(1)}, s32[384]{0:T(512)}, u32[]{:S(2)}) copy-start(s32[384]{0:T(512)} %param.13) | copy-start | bytes 4612
  0.9 0.8 %copy-start.1 = (f32[1,1536]{1,0:T(1,128)S(1)}, f32[1,1536]{1,0:T(1,128)}, u32[]{:S(2)}) copy-start(f32[1,1536]{1,0:T(1,128)} %gate_hbm.7) | copy-start | bytes 18436
  1.6 0.7 %copy-start.2 = (f32[1,128]{1,0:T(1,128)S(1)}, f32[1,128]{1,0:T(1,128)}, u32[]{:S(2)}) copy-start(f32[1,128]{1,0:T(1,128)} %qgain_hbm.7) | copy-start | bytes 1540
  1.6 0.7 %copy-start.3 = (f32[1,128]{1,0:T(1,128)S(1)}, f32[1,128]{1,0:T(1,128)}, u32[]{:S(2)}) copy-start(f32[1,128]{1,0:T(1,128)} %kgain_hbm.7) | copy-start | bytes 1540
  3.4 12.8 %collective-permute-start.3 = (bf16[256,384]{1,0:T(8,128)(2,1)S(1)}, bf16[256,384]{1,0:T(8,128)(2,1)S(1)}, u32[]{:S(2)}, u32[]{:S(2)}) collective-permute-start(bf16[256,384]{1,0:T(8,128)(2,1)S(1)} %shard_map.76), channel_id=1, source_target_pairs={{0,0},{1,2},{2,1},{3,3},{4,4},{5,6},{6,5},{7,7},{8,8},{9,10},{10,9... | collective-permute-start | bytes 589832 | tf_op jit(solution)/shard_map/ppermute | solution.py:115
  9.0 14.7 %collective-permute-start = (bf16[240,384]{1,0:T(8,128)(2,1)S(1)}, bf16[240,384]{1,0:T(8,128)(2,1)S(1)}, u32[]{:S(2)}, u32[]{:S(2)}) collective-permute-start(bf16[240,384]{1,0:T(8,128)(2,1)S(1)} %shard_map.73), channel_id=1, source_target_pairs={{0,8},{1,10},{2,9},{3,11},{4,12},{5,14},{6,13},{7,15},{8,0},{9,2},... | collective-permute-start | bytes 552968 | tf_op jit(solution)/shard_map/ppermute | solution.py:115
  12.2 15.4 %copy-start = (s32[384,1]{1,0:T(8,128)S(1)}, s32[384,1]{1,0:T(8,128)}, u32[]{:S(2)}) copy-start(s32[384,1]{1,0:T(8,128)} %reshape.8.refs_1_.query_ids) | copy-start | bytes 4612
  12.2 11.5 %collective-permute-start.1 = (bf16[240,384]{1,0:T(8,128)(2,1)S(1)}, bf16[240,384]{1,0:T(8,128)(2,1)S(1)}, u32[]{:S(2)}, u32[]{:S(2)}) collective-permute-start(bf16[240,384]{1,0:T(8,128)(2,1)S(1)} %shard_map.74), channel_id=1, source_target_pairs={{0,12},{1,14},{2,13},{3,15},{4,8},{5,10},{6,9},{7,11},{8,4},{9,6},... | collective-permute-start | bytes 552968 | tf_op jit(solution)/shard_map/ppermute | solution.py:115
  15.9 8.6 %collective-permute-start.2 = (bf16[240,384]{1,0:T(8,128)(2,1)S(1)}, bf16[240,384]{1,0:T(8,128)(2,1)S(1)}, u32[]{:S(2)}, u32[]{:S(2)}) collective-permute-start(bf16[240,384]{1,0:T(8,128)(2,1)S(1)} %shard_map.75), channel_id=1, source_target_pairs={{0,4},{1,6},{2,5},{3,7},{4,0},{5,2},{6,1},{7,3},{8,12},{9,14},{10,... | collective-permute-start | bytes 552968 | tf_op jit(solution)/shard_map/ppermute | solution.py:115
  16.2 11.4 %collective-permute-start.7 = (bf16[256,384]{1,0:T(8,128)(2,1)S(1)}, bf16[256,384]{1,0:T(8,128)(2,1)S(1)}, u32[]{:S(2)}, u32[]{:S(2)}) collective-permute-start(bf16[256,384]{1,0:T(8,128)(2,1)S(1)} %collective-permute-done.3.refs_3_), channel_id=1, source_target_pairs={{0,1},{1,0},{2,3},{3,2},{4,5},{5,4},{6,7},{7,6},{8,9},{9,8},{10,11... | collective-permute-start | bytes 589832 | tf_op jit(solution)/shard_map/ppermute | solution.py:288
  23.7 2.7 %collective-permute-start.4 = (bf16[240,384]{1,0:T(8,128)(2,1)S(1)}, bf16[240,384]{1,0:T(8,128)(2,1)S(1)}, u32[]{:S(2)}, u32[]{:S(2)}) collective-permute-start(bf16[240,384]{1,0:T(8,128)(2,1)S(1)} %collective-permute-done.refs_0_), channel_id=1, source_target_pairs={{0,1},{1,0},{2,3},{3,2},{4,5},{5,4},{6,7},{7,6},{8,9},{9,8},{10,11... | collective-permute-start | bytes 552968 | tf_op jit(solution)/shard_map/ppermute | solution.py:288
  23.7 2.7 %collective-permute-start.5 = (bf16[240,384]{1,0:T(8,128)(2,1)S(1)}, bf16[240,384]{1,0:T(8,128)(2,1)S(1)}, u32[]{:S(2)}, u32[]{:S(2)}) collective-permute-start(bf16[240,384]{1,0:T(8,128)(2,1)S(1)} %collective-permute-done.1.refs_1_), channel_id=1, source_target_pairs={{0,1},{1,0},{2,3},{3,2},{4,5},{5,4},{6,7},{7,6},{8,9},{9,8},{10,11... | collective-permute-start | bytes 552968 | tf_op jit(solution)/shard_map/ppermute | solution.py:288
  24.5 3.0 %collective-permute-start.6 = (bf16[240,384]{1,0:T(8,128)(2,1)S(1)}, bf16[240,384]{1,0:T(8,128)(2,1)S(1)}, u32[]{:S(2)}, u32[]{:S(2)}) collective-permute-start(bf16[240,384]{1,0:T(8,128)(2,1)S(1)} %collective-permute-done.2.refs_2_), channel_id=1, source_target_pairs={{0,1},{1,0},{2,3},{3,2},{4,5},{5,4},{6,7},{7,6},{8,9},{9,8},{10,11... | collective-permute-start | bytes 552968 | tf_op jit(solution)/shard_map/ppermute | solution.py:288
  29.9 8.0 %collective-permute-start.8 = (bf16[96,384]{1,0:T(8,128)(2,1)S(1)}, bf16[96,384]{1,0:T(8,128)(2,1)S(1)}, u32[]{:S(2)}, u32[]{:S(2)}) collective-permute-start(bf16[96,384]{1,0:T(8,128)(2,1)S(1)} %get-tuple-element.9), channel_id=1, source_target_pairs={{0,8},{1,10},{2,9},{3,11},{4,12},{5,14},{6,13},{7,15},{8,0},{9,2},... | collective-permute-start | bytes 221192 | tf_op jit(solution)/shard_map/ppermute | solution.py:115
  33.0 7.3 %collective-permute-start.9 = (bf16[96,384]{1,0:T(8,128)(2,1)S(1)}, bf16[96,384]{1,0:T(8,128)(2,1)S(1)}, u32[]{:S(2)}, u32[]{:S(2)}) collective-permute-start(bf16[96,384]{1,0:T(8,128)(2,1)S(1)} %get-tuple-element.10), channel_id=1, source_target_pairs={{0,12},{1,14},{2,13},{3,15},{4,8},{5,10},{6,9},{7,11},{8,4},{9,6},... | collective-permute-start | bytes 221192 | tf_op jit(solution)/shard_map/ppermute | solution.py:115
  34.6 6.4 %collective-permute-start.10 = (bf16[96,384]{1,0:T(8,128)(2,1)S(1)}, bf16[96,384]{1,0:T(8,128)(2,1)S(1)}, u32[]{:S(2)}, u32[]{:S(2)}) collective-permute-start(bf16[96,384]{1,0:T(8,128)(2,1)S(1)} %get-tuple-element.11), channel_id=1, source_target_pairs={{0,4},{1,6},{2,5},{3,7},{4,0},{5,2},{6,1},{7,3},{8,12},{9,14},{10,... | collective-permute-start | bytes 221192 | tf_op jit(solution)/shard_map/ppermute | solution.py:115
  34.7 6.8 %collective-permute-start.11 = (bf16[96,384]{1,0:T(8,128)(2,1)S(1)}, bf16[96,384]{1,0:T(8,128)(2,1)S(1)}, u32[]{:S(2)}, u32[]{:S(2)}) collective-permute-start(bf16[96,384]{1,0:T(8,128)(2,1)S(1)} %get-tuple-element.12), channel_id=1, source_target_pairs={{0,0},{1,2},{2,1},{3,3},{4,4},{5,6},{6,5},{7,7},{8,8},{9,10},{10,9... | collective-permute-start | bytes 221192 | tf_op jit(solution)/shard_map/ppermute | solution.py:115
where the time goes:
time: 42.6 us; the launch traced here: 42.3 us
  starting transfers between devices  19.2 us (45%)
  waiting for transfers between devices  13.2 us (31%)
  Pallas kernels  7.45 us (17%)
  local copies, waits for them, and re-layouts  2.24 us (5%)
    ppermute x8, starting transfers between devices, swapped(): return lax.ppermute(array, MESH_TAIL, pairs)  16.8 us
    ppermute x8, waiting for transfers between devices, swapped(): return lax.ppermute(array, MESH_TAIL, pairs)  12.2 us
    pallas_call x4, Pallas kernels, pack(): pl.pallas_call(functools.partial(pack_kernel, offset), out_shape=jax.Shap...  4.31 us
    ppermute x4, starting transfers between devices, by_heads(): other.append(lax.ppermute(payload, 'head', [(0, 1), (1, 0)]))  2.49 us
    pallas_call x1, Pallas kernels, by_heads(): pl.pallas_call(functools.partial(attend_kernel, offsets, rows), out_shape...  2.39 us
    unnamed x10, local copies, waits for them, and re-layouts  1.36 us
    ppermute x4, waiting for transfers between devices, by_heads(): other.append(lax.ppermute(payload, 'head', [(0, 1), (1, 0)]))  1.06 us
  transfers between devices with their start and end apart: 12, of which 7 were waited for; matrix products, arithmetic and copies ran while one was open for 0% of the time, Pallas kernels for 8%

commit v1 on v0

--- a/solution.py
+++ b/solution.py
@@ -12,7 +12,6 @@
 HEAD_DIM = 128
 PART_ROWS = 16
 BLOCKED = -1e30
-PACK_GRANT = 54880 << 10
 
 
 def passed_along(shard, axis, by):
@@ -129,7 +128,7 @@
     return [part.astype(jnp.float32) for part in (high, middle, low)]
 
 
-def pack_kernel(offset, key_hbm, value_hbm, hidden_hbm, qgain_hbm, kgain_hbm, gate_hbm, *refs):
+def pack_kernel(offset, key_hbm, value_hbm, hidden_hbm, kgain_hbm, *refs):
     out, kgain, qgain, gate, sems = refs[-5:]
     rows = key_hbm.shape[0]
     width = out.shape[1]
@@ -144,7 +143,7 @@
         (hidden_hbm.at[pl.ds(first, half), columns], out.at[pl.ds(2 * rows, half)]),
     ]
     if offset == 0:
-        moves += [(qgain_hbm, qgain), (gate_hbm.at[:, columns], gate)]
+        moves += [(refs[0], qgain), (refs[1].at[:, columns], gate)]
     copies = []
     for which, (source, target) in enumerate(moves):
         copy = pltpu.make_async_copy(source, target, sems.at[which])
@@ -265,10 +264,14 @@
     def pack(at, *after):
         offset = offsets[at]
         size = 2 * rows + half + (PART_ROWS if offset == 0 else 0)
+        sources = [key_cache[0], value_cache[0], hidden_in, key_gain]
+        if offset == 0:
+            sources += [query_gain, out_gate]
+        sources = [pltpu.with_memory_space_constraint(source, pltpu.HBM) for source in sources]
         payload = pl.pallas_call(
             functools.partial(pack_kernel, offset),
             out_shape=jax.ShapeDtypeStruct((size, width), jnp.bfloat16),
-            in_specs=[hbm] * 6 + [anywhere] * len(after),
+            in_specs=[hbm] * len(sources) + [anywhere] * len(after),
             out_specs=vmem,
             scratch_shapes=[
                 pltpu.VMEM((1, HEAD_DIM), jnp.float32),
@@ -276,8 +279,8 @@
                 pltpu.VMEM((1, width), jnp.float32),
                 pltpu.SemaphoreType.DMA((6,)),
             ],
-            compiler_params=grant(PACK_GRANT),
-        )(key_cache[0], value_cache[0], hidden_in, query_gain, key_gain, out_gate, *after)
+            compiler_params=grant(2 << 20),
+        )(*sources, *after)
         return payload
 
     own, other = [], []
@@ -311,7 +314,7 @@
 
 def send_order(blocks):
     far = blocks // 2
-    return tuple(range(far, blocks)) + tuple(reversed(range(far)))
+    return (far, *range(1, far), *range(far + 1, blocks), 0)
 
 
 def solution(mesh):

time: 42.6 us -> 40.6 us (0.953)
  local copies, waits for them, and re-layouts: 2.24 us -> 0.87 us
  waiting for transfers between devices: 13.2 us -> 12.2 us
    ppermute x8, starting transfers between devices: 16.8 us -> 19.1 us  [swapped(): return lax.ppermute(array, MESH_TAIL, pairs)]
    ppermute x4, starting transfers between devices: 2.49 us -> 0.45 us  [by_heads(): other.append(lax.ppermute(payload, 'head', [(0, 1), (1, 0)]))]
    ppermute x8, waiting for transfers between devices: 12.2 us -> 10.8 us  [swapped(): return lax.ppermute(array, MESH_TAIL, pairs)]
    reshape x2, local copies, waits for them, and re-layouts: 0.8 us -> 0.11 us  [by_heads(): ids_row, ids_column = (ids.reshape(1, total), ids.reshape(total, 1))]
    unnamed x10 -> x2, local copies, waits for them, and re-layouts: 1.36 us -> 0.68 us
  transfers between devices with their start and end apart: 12 -> 12, of which waited for: 7 -> 6; matrix products, arithmetic and copies ran while one was open for 0% -> 0% of each run, Pallas kernels for 8% -> 8%
where the time goes in v1:
time: 40.6 us; the launch traced here: 40.3 us
  starting transfers between devices  19.6 us (48%)
  waiting for transfers between devices  12.2 us (30%)
  Pallas kernels  7.47 us (18%)
  local copies, waits for them, and re-layouts  0.87 us (2%)
    ppermute x8, starting transfers between devices, swapped(): return lax.ppermute(array, MESH_TAIL, pairs)  19.1 us
    ppermute x8, waiting for transfers between devices, swapped(): return lax.ppermute(array, MESH_TAIL, pairs)  10.8 us
    pallas_call x4, Pallas kernels, pack(): pl.pallas_call(functools.partial(pack_kernel, offset), out_shape=jax.Shap...  4.32 us
    pallas_call x1, Pallas kernels, by_heads(): pl.pallas_call(functools.partial(attend_kernel, offsets, rows), out_shape...  2.39 us
    ppermute x4, waiting for transfers between devices, by_heads(): other.append(lax.ppermute(payload, 'head', [(0, 1), (1, 0)]))  1.42 us
  transfers between devices with their start and end apart: 12, of which 6 were waited for; matrix products, arithmetic and copies ran while one was open for 0% of the time, Pallas kernels for 8%

profile of v1, /device:TPU:1, one launch (start us, length us, event | category | flops | bytes accessed | tf_op | source)
XLA Modules:
  0.0 40.3 jit_solution(3575373184943670562)
XLA Ops:
  0.0 0.7 %copy-done = s32[384]{0:T(512)S(1)} copy-done((s32[384]{0:T(512)S(1)}, s32[384]{0:T(512)}, u32[]{:S(2)}) %copy-start) | copy-done | bytes 1560
  0.7 0.1 fusion
  0.8 0.1 pad_add_fusion
  0.9 0.1 reshape.8.refs_3_.query_ids
  1.0 1.1 %shard_map.76 = bf16[256,384]{1,0:T(8,128)(2,1)S(1)} custom-call(bf16[96,1536]{1,0:T(8,128)(2,1)} %bitcast.3, bf16[96,1536]{1,0:T(8,128)(2,1)} %bitcast.7, bf16[96,1536]{1,0:T(8,128)(2,1)} %hidden_hbm.7, f32[1,128]{1,0:T(1,128)} %kgain_hbm.7, f32[1,128]{1,0:T(1,128)} %refs_0_.1, f32[1,1536]{1,0:T(1,128)} %refs_1_.1, s32[1,384]{1,0:T(1,128)S(1)} %reshape.6.refs_2_.key_ids, ...), custom_call_target="tpu_custom_call" | custom-call | tf_op jit(solution)/shard_map/pallas_call | solution.py:271
  2.1 4.5 %collective-permute-start.3 = (bf16[256,384]{1,0:T(8,128)(2,1)S(1)}, bf16[256,384]{1,0:T(8,128)(2,1)S(1)}, u32[]{:S(2)}, u32[]{:S(2)}) collective-permute-start(bf16[256,384]{1,0:T(8,128)(2,1)S(1)} %shard_map.76), channel_id=1, source_target_pairs={{0,0},{1,2},{2,1},{3,3},{4,4},{5,6},{6,5},{7,7},{8,8},{9,10},{10,9... | collective-permute-start | bytes 589832 | tf_op jit(solution)/shard_map/ppermute | solution.py:114
  6.6 1.1 %shard_map.73 = bf16[240,384]{1,0:T(8,128)(2,1)S(1)} custom-call(bf16[96,1536]{1,0:T(8,128)(2,1)} %bitcast.4, bf16[96,1536]{1,0:T(8,128)(2,1)} %bitcast.8, bf16[96,1536]{1,0:T(8,128)(2,1)} %hidden_hbm.7, f32[1,128]{1,0:T(1,128)} %kgain_hbm.7), custom_call_target="tpu_custom_call" | custom-call | tf_op jit(solution)/shard_map/pallas_call | solution.py:271
  7.7 2.1 %collective-permute-start = (bf16[240,384]{1,0:T(8,128)(2,1)S(1)}, bf16[240,384]{1,0:T(8,128)(2,1)S(1)}, u32[]{:S(2)}, u32[]{:S(2)}) collective-permute-start(bf16[240,384]{1,0:T(8,128)(2,1)S(1)} %shard_map.73), channel_id=1, source_target_pairs={{0,8},{1,10},{2,9},{3,11},{4,12},{5,14},{6,13},{7,15},{8,0},{9,2},... | collective-permute-start | bytes 552968 | tf_op jit(solution)/shard_map/ppermute | solution.py:114
  9.8 1.1 %shard_map.74 = bf16[240,384]{1,0:T(8,128)(2,1)S(1)} custom-call(bf16[96,1536]{1,0:T(8,128)(2,1)} %bitcast.5, bf16[96,1536]{1,0:T(8,128)(2,1)} %bitcast.9, bf16[96,1536]{1,0:T(8,128)(2,1)} %hidden_hbm.7, f32[1,128]{1,0:T(1,128)} %kgain_hbm.7), custom_call_target="tpu_custom_call" | custom-call | tf_op jit(solution)/shard_map/pallas_call | solution.py:271
  10.9 2.8 %collective-permute-start.1 = (bf16[240,384]{1,0:T(8,128)(2,1)S(1)}, bf16[240,384]{1,0:T(8,128)(2,1)S(1)}, u32[]{:S(2)}, u32[]{:S(2)}) collective-permute-start(bf16[240,384]{1,0:T(8,128)(2,1)S(1)} %shard_map.74), channel_id=1, source_target_pairs={{0,4},{1,6},{2,5},{3,7},{4,0},{5,2},{6,1},{7,3},{8,12},{9,14},{10,... | collective-permute-start | bytes 552968 | tf_op jit(solution)/shard_map/ppermute | solution.py:114
  13.7 1.1 %shard_map.75 = bf16[240,384]{1,0:T(8,128)(2,1)S(1)} custom-call(bf16[96,1536]{1,0:T(8,128)(2,1)} %bitcast.6, bf16[96,1536]{1,0:T(8,128)(2,1)} %bitcast.10, bf16[96,1536]{1,0:T(8,128)(2,1)} %hidden_hbm.7, f32[1,128]{1,0:T(1,128)} %kgain_hbm.7), custom_call_target="tpu_custom_call" | custom-call | tf_op jit(solution)/shard_map/pallas_call | solution.py:271
  14.9 5.5 %collective-permute-done.refs_0_ = bf16[240,384]{1,0:T(8,128)(2,1)S(1)} collective-permute-done((bf16[240,384]{1,0:T(8,128)(2,1)S(1)}, bf16[240,384]{1,0:T(8,128)(2,1)S(1)}, u32[]{:S(2)}, u32[]{:S(2)}) %collective-permute-start) | collective-permute-done | bytes 184352 | tf_op jit(solution)/shard_map/ppermute | solution.py:114
  20.4 0.1 collective-permute-done.1.refs_1_
  20.6 0.4 collective-permute-start.5
  21.0 1.6 %collective-permute-done.2.refs_2_ = bf16[240,384]{1,0:T(8,128)(2,1)S(1)} collective-permute-done((bf16[240,384]{1,0:T(8,128)(2,1)S(1)}, bf16[240,384]{1,0:T(8,128)(2,1)S(1)}, u32[]{:S(2)}, u32[]{:S(2)}) %collective-permute-start.2) | collective-permute-done | bytes 184352 | tf_op jit(solution)/shard_map/ppermute | solution.py:114
  22.6 1.4 %collective-permute-done.6.refs_6_ = bf16[240,384]{1,0:T(8,128)(2,1)S(1)} collective-permute-done((bf16[240,384]{1,0:T(8,128)(2,1)S(1)}, bf16[240,384]{1,0:T(8,128)(2,1)S(1)}, u32[]{:S(2)}, u32[]{:S(2)}) %collective-permute-start.6) | collective-permute-done | bytes 184352 | tf_op jit(solution)/shard_map/ppermute | solution.py:291
  24.0 2.4 %attend.1 = (bf16[96,384]{1,0:T(8,128)(2,1)S(1)}, bf16[96,384]{1,0:T(8,128)(2,1)S(1)}, bf16[96,384]{1,0:T(8,128)(2,1)S(1)}, bf16[96,384]{1,0:T(8,128)(2,1)S(1)}) custom-call(s32[1,384]{1,0:T(1,128)S(1)} %reshape.6.refs_2_.key_ids, s32[384,1]{1,0:T(8,128)S(1)} %reshape.8.refs_3_.query_ids, bf16[240,384]{1,0:T(8,128)(2,1)S(1)} %collective-permute-done.refs_0_, ...), custom_call_target="tpu_custom_call" | custom-call | tf_op jit(solution)/shard_map/attend/pallas_call | solution.py:292
  26.4 5.0 %collective-permute-start.8 = (bf16[96,384]{1,0:T(8,128)(2,1)S(1)}, bf16[96,384]{1,0:T(8,128)(2,1)S(1)}, u32[]{:S(2)}, u32[]{:S(2)}) collective-permute-start(bf16[96,384]{1,0:T(8,128)(2,1)S(1)} %get-tuple-element.9), channel_id=1, source_target_pairs={{0,8},{1,10},{2,9},{3,11},{4,12},{5,14},{6,13},{7,15},{8,0},{9,2},... | collective-permute-start | bytes 221192 | tf_op jit(solution)/shard_map/ppermute | solution.py:114
  31.4 0.1 collective-permute-start.9
  31.6 2.3 %collective-permute-start.10 = (bf16[96,384]{1,0:T(8,128)(2,1)S(1)}, bf16[96,384]{1,0:T(8,128)(2,1)S(1)}, u32[]{:S(2)}, u32[]{:S(2)}) collective-permute-start(bf16[96,384]{1,0:T(8,128)(2,1)S(1)} %get-tuple-element.11), channel_id=1, source_target_pairs={{0,12},{1,14},{2,13},{3,15},{4,8},{5,10},{6,9},{7,11},{8,4},{9,6},... | collective-permute-start | bytes 221192 | tf_op jit(solution)/shard_map/ppermute | solution.py:114
  33.9 2.2 %collective-permute-start.11 = (bf16[96,384]{1,0:T(8,128)(2,1)S(1)}, bf16[96,384]{1,0:T(8,128)(2,1)S(1)}, u32[]{:S(2)}, u32[]{:S(2)}) collective-permute-start(bf16[96,384]{1,0:T(8,128)(2,1)S(1)} %get-tuple-element.12), channel_id=1, source_target_pairs={{0,0},{1,2},{2,1},{3,3},{4,4},{5,6},{6,5},{7,7},{8,8},{9,10},{10,9... | collective-permute-start | bytes 221192 | tf_op jit(solution)/shard_map/ppermute | solution.py:114
  36.1 2.7 %collective-permute-done.9.refs_1_ = bf16[96,384]{1,0:T(8,128)(2,1)S(1)} collective-permute-done((bf16[96,384]{1,0:T(8,128)(2,1)S(1)}, bf16[96,384]{1,0:T(8,128)(2,1)S(1)}, u32[]{:S(2)}, u32[]{:S(2)}) %collective-permute-start.9) | collective-permute-done | bytes 73760 | tf_op jit(solution)/shard_map/ppermute | solution.py:114
  38.8 0.8 %collective-permute-done.11.refs_3_ = bf16[96,384]{1,0:T(8,128)(2,1)S(1)} collective-permute-done((bf16[96,384]{1,0:T(8,128)(2,1)S(1)}, bf16[96,384]{1,0:T(8,128)(2,1)S(1)}, u32[]{:S(2)}, u32[]{:S(2)}) %collective-permute-start.11) | collective-permute-done | bytes 73760 | tf_op jit(solution)/shard_map/ppermute | solution.py:114
  39.5 0.8 %join.1 = bf16[96,1536]{1,0:T(8,128)(2,1)} custom-call(bf16[96,384]{1,0:T(8,128)(2,1)S(1)} %collective-permute-done.8.refs_0_, bf16[96,384]{1,0:T(8,128)(2,1)S(1)} %collective-permute-done.9.refs_1_, bf16[96,384]{1,0:T(8,128)(2,1)S(1)} %collective-permute-done.10.refs_2_, bf16[96,384]{1,0:T(8,128)(2,1)S(1)} %collective-permute-done.11.refs_3_), custom_call_target="tpu_custom_call" | custom-call | tf_op jit(solution)/shard_map/join/pallas_call | solution.py:304
  (12 shorter events, 0.2 us)
Async XLA Ops:
  0.0 0.7 %copy-start = (s32[384]{0:T(512)S(1)}, s32[384]{0:T(512)}, u32[]{:S(2)}) copy-start(s32[384]{0:T(512)} %param.13) | copy-start | bytes 4612
  2.1 12.7 %collective-permute-start.3 = (bf16[256,384]{1,0:T(8,128)(2,1)S(1)}, bf16[256,384]{1,0:T(8,128)(2,1)S(1)}, u32[]{:S(2)}, u32[]{:S(2)}) collective-permute-start(bf16[256,384]{1,0:T(8,128)(2,1)S(1)} %shard_map.76), channel_id=1, source_target_pairs={{0,0},{1,2},{2,1},{3,3},{4,4},{5,6},{6,5},{7,7},{8,8},{9,10},{10,9... | collective-permute-start | bytes 589832 | tf_op jit(solution)/shard_map/ppermute | solution.py:114
  7.7 12.8 %collective-permute-start = (bf16[240,384]{1,0:T(8,128)(2,1)S(1)}, bf16[240,384]{1,0:T(8,128)(2,1)S(1)}, u32[]{:S(2)}, u32[]{:S(2)}) collective-permute-start(bf16[240,384]{1,0:T(8,128)(2,1)S(1)} %shard_map.73), channel_id=1, source_target_pairs={{0,8},{1,10},{2,9},{3,11},{4,12},{5,14},{6,13},{7,15},{8,0},{9,2},... | collective-permute-start | bytes 552968 | tf_op jit(solution)/shard_map/ppermute | solution.py:114
  10.9 9.7 %collective-permute-start.1 = (bf16[240,384]{1,0:T(8,128)(2,1)S(1)}, bf16[240,384]{1,0:T(8,128)(2,1)S(1)}, u32[]{:S(2)}, u32[]{:S(2)}) collective-permute-start(bf16[240,384]{1,0:T(8,128)(2,1)S(1)} %shard_map.74), channel_id=1, source_target_pairs={{0,4},{1,6},{2,5},{3,7},{4,0},{5,2},{6,1},{7,3},{8,12},{9,14},{10,... | collective-permute-start | bytes 552968 | tf_op jit(solution)/shard_map/ppermute | solution.py:114
  14.7 7.8 %collective-permute-start.2 = (bf16[240,384]{1,0:T(8,128)(2,1)S(1)}, bf16[240,384]{1,0:T(8,128)(2,1)S(1)}, u32[]{:S(2)}, u32[]{:S(2)}) collective-permute-start(bf16[240,384]{1,0:T(8,128)(2,1)S(1)} %shard_map.75), channel_id=1, source_target_pairs={{0,12},{1,14},{2,13},{3,15},{4,8},{5,10},{6,9},{7,11},{8,4},{9,6},... | collective-permute-start | bytes 552968 | tf_op jit(solution)/shard_map/ppermute | solution.py:114
  14.8 9.2 %collective-permute-start.7 = (bf16[256,384]{1,0:T(8,128)(2,1)S(1)}, bf16[256,384]{1,0:T(8,128)(2,1)S(1)}, u32[]{:S(2)}, u32[]{:S(2)}) collective-permute-start(bf16[256,384]{1,0:T(8,128)(2,1)S(1)} %collective-permute-done.3.refs_3_), channel_id=1, source_target_pairs={{0,1},{1,0},{2,3},{3,2},{4,5},{5,4},{6,7},{7,6},{8,9},{9,8},{10,11... | collective-permute-start | bytes 589832 | tf_op jit(solution)/shard_map/ppermute | solution.py:291
  20.4 2.1 %collective-permute-start.4 = (bf16[240,384]{1,0:T(8,128)(2,1)S(1)}, bf16[240,384]{1,0:T(8,128)(2,1)S(1)}, u32[]{:S(2)}, u32[]{:S(2)}) collective-permute-start(bf16[240,384]{1,0:T(8,128)(2,1)S(1)} %collective-permute-done.refs_0_), channel_id=1, source_target_pairs={{0,1},{1,0},{2,3},{3,2},{4,5},{5,4},{6,7},{7,6},{8,9},{9,8},{10,11... | collective-permute-start | bytes 552968 | tf_op jit(solution)/shard_map/ppermute | solution.py:291
  20.6 2.0 %collective-permute-start.5 = (bf16[240,384]{1,0:T(8,128)(2,1)S(1)}, bf16[240,384]{1,0:T(8,128)(2,1)S(1)}, u32[]{:S(2)}, u32[]{:S(2)}) collective-permute-start(bf16[240,384]{1,0:T(8,128)(2,1)S(1)} %collective-permute-done.1.refs_1_), channel_id=1, source_target_pairs={{0,1},{1,0},{2,3},{3,2},{4,5},{5,4},{6,7},{7,6},{8,9},{9,8},{10,11... | collective-permute-start | bytes 552968 | tf_op jit(solution)/shard_map/ppermute | solution.py:291
  22.6 1.4 %collective-permute-start.6 = (bf16[240,384]{1,0:T(8,128)(2,1)S(1)}, bf16[240,384]{1,0:T(8,128)(2,1)S(1)}, u32[]{:S(2)}, u32[]{:S(2)}) collective-permute-start(bf16[240,384]{1,0:T(8,128)(2,1)S(1)} %collective-permute-done.2.refs_2_), channel_id=1, source_target_pairs={{0,1},{1,0},{2,3},{3,2},{4,5},{5,4},{6,7},{7,6},{8,9},{9,8},{10,11... | collective-permute-start | bytes 552968 | tf_op jit(solution)/shard_map/ppermute | solution.py:291
  26.4 9.7 %collective-permute-start.8 = (bf16[96,384]{1,0:T(8,128)(2,1)S(1)}, bf16[96,384]{1,0:T(8,128)(2,1)S(1)}, u32[]{:S(2)}, u32[]{:S(2)}) collective-permute-start(bf16[96,384]{1,0:T(8,128)(2,1)S(1)} %get-tuple-element.9), channel_id=1, source_target_pairs={{0,8},{1,10},{2,9},{3,11},{4,12},{5,14},{6,13},{7,15},{8,0},{9,2},... | collective-permute-start | bytes 221192 | tf_op jit(solution)/shard_map/ppermute | solution.py:114
  31.4 7.3 %collective-permute-start.9 = (bf16[96,384]{1,0:T(8,128)(2,1)S(1)}, bf16[96,384]{1,0:T(8,128)(2,1)S(1)}, u32[]{:S(2)}, u32[]{:S(2)}) collective-permute-start(bf16[96,384]{1,0:T(8,128)(2,1)S(1)} %get-tuple-element.10), channel_id=1, source_target_pairs={{0,4},{1,6},{2,5},{3,7},{4,0},{5,2},{6,1},{7,3},{8,12},{9,14},{10,... | collective-permute-start | bytes 221192 | tf_op jit(solution)/shard_map/ppermute | solution.py:114
  31.6 7.2 %collective-permute-start.10 = (bf16[96,384]{1,0:T(8,128)(2,1)S(1)}, bf16[96,384]{1,0:T(8,128)(2,1)S(1)}, u32[]{:S(2)}, u32[]{:S(2)}) collective-permute-start(bf16[96,384]{1,0:T(8,128)(2,1)S(1)} %get-tuple-element.11), channel_id=1, source_target_pairs={{0,12},{1,14},{2,13},{3,15},{4,8},{5,10},{6,9},{7,11},{8,4},{9,6},... | collective-permute-start | bytes 221192 | tf_op jit(solution)/shard_map/ppermute | solution.py:114
  33.9 5.7 %collective-permute-start.11 = (bf16[96,384]{1,0:T(8,128)(2,1)S(1)}, bf16[96,384]{1,0:T(8,128)(2,1)S(1)}, u32[]{:S(2)}, u32[]{:S(2)}) collective-permute-start(bf16[96,384]{1,0:T(8,128)(2,1)S(1)} %get-tuple-element.12), channel_id=1, source_target_pairs={{0,0},{1,2},{2,1},{3,3},{4,4},{5,6},{6,5},{7,7},{8,8},{9,10},{10,9... | collective-permute-start | bytes 221192 | tf_op jit(solution)/shard_map/ppermute | solution.py:114

commit v2 on v1

--- a/solution.py
+++ b/solution.py
@@ -103,13 +103,14 @@
 MESH_TAIL = ("tm", "segment", "head")
 
 
-def swapped(array, offset, blocks):
+def swapped(array, offset, blocks, own=True):
     at = lambda t, s, c: (t * 2 + s) * 2 + c
     pairs = [
         (at(t, s, c), at(t ^ offset, c, s))
         for t in range(blocks)
         for s in range(2)
         for c in range(2)
+        if own or offset or s != c
     ]
     return lax.ppermute(array, MESH_TAIL, pairs)
 
@@ -167,6 +168,12 @@
         out[pl.ds(2 * rows + half, PART_ROWS), :] = table.astype(jnp.bfloat16)
 
 
+def mask_kernel(key_ids, query_ids, bias):
+    keys_row, queries_column = key_ids[...], query_ids[...]
+    allowed = (keys_row <= queries_column) & (keys_row >= queries_column - 2)
+    bias[...] = jnp.where(allowed, 0.0, BLOCKED)
+
+
 def layer_rows(current, keys, values, bias, query_gain, gate):
     scale = 2.0 / math.sqrt(HEAD_DIM) * math.log2(math.e)
     queries = normed(current, query_gain)
@@ -180,48 +187,55 @@
     return (current.astype(jnp.float32) + gate * mixture).astype(jnp.bfloat16)
 
 
-def attend_kernel(offsets, rows, key_ids, query_ids, *refs):
+def attend_kernel(offsets, rows, *refs):
     count = len(offsets)
+    bias_ref, refs = refs[0], refs[1:]
     own, other, outs = refs[:count], refs[count : 2 * count], refs[2 * count : 3 * count]
-    bias_ref = refs[3 * count]
     width = outs[0].shape[1]
     half = rows // 2
-    core = lax.axis_index("head")
-    keys_row, queries_column = key_ids[...], query_ids[...]
-    allowed = (keys_row <= queries_column) & (keys_row >= queries_column - 2)
-    bias_ref[...] = jnp.where(allowed, 0.0, BLOCKED)
 
     def run(first, second, last):
-        for head in range(width // HEAD_DIM):
-            lanes = pl.ds(head * HEAD_DIM, HEAD_DIM)
-            bias = bias_ref[...]
-
-            def part(refs_, start, size):
-                return jnp.concatenate([ref[pl.ds(start, size), lanes] for ref in refs_], axis=0)
-
-            def table(refs_, line):
-                at = offsets.index(0)
-                block = refs_[at][pl.ds(2 * rows + half, PART_ROWS), lanes].astype(jnp.float32)
-                return block[line : line + 1] + (
-                    block[line + 1 : line + 2] + block[line + 2 : line + 3]
-                )
-
-            current = jnp.concatenate(
-                [ref[pl.ds(2 * rows, half), lanes] for at in range(count) for ref in (first[at], second[at])],
+        def part(refs_, start, size, lanes):
+            return jnp.concatenate([ref[pl.ds(start, size), lanes] for ref in refs_], axis=0)
+
+        def table(refs_, line, lanes):
+            block = refs_[offsets.index(0)][pl.ds(2 * rows + half, PART_ROWS), lanes]
+            block = block.astype(jnp.float32)
+            return block[line : line + 1] + (
+                block[line + 1 : line + 2] + block[line + 2 : line + 3]
+            )
+
+        heads = range(width // HEAD_DIM)
+        lanes_of = [pl.ds(head * HEAD_DIM, HEAD_DIM) for head in heads]
+        current = [
+            jnp.concatenate(
+                [
+                    ref[pl.ds(2 * rows, half), lanes]
+                    for at in range(count)
+                    for ref in (first[at], second[at])
+                ],
                 axis=0,
             )
-            for section in range(last + 1):
-                source = (first, second)[section]
-                current = layer_rows(
-                    current,
-                    part(source, 0, rows),
-                    part(source, rows, rows),
+            for lanes in lanes_of
+        ]
+        bias = bias_ref[...]
+        for section in range(last + 1):
+            source = (first, second)[section]
+            for head in heads:
+                lanes = lanes_of[head]
+                current[head] = layer_rows(
+                    current[head],
+                    part(source, 0, rows, lanes),
+                    part(source, rows, rows, lanes),
                     bias,
-                    table(source, 3),
-                    table(source, 0),
+                    table(source, 3, lanes),
+                    table(source, 0, lanes),
                 )
+        for head in heads:
             for at in range(count):
-                outs[at][:, lanes] = current[at * rows : (at + 1) * rows]
+                outs[at][:, lanes_of[head]] = current[head][at * rows : (at + 1) * rows]
+
+    core = lax.axis_index("head")
 
     @pl.when(core == 0)
     def _():
@@ -232,12 +246,31 @@
         run(other, own, 1)
 
 
-def join_kernel(offsets, *refs):
-    out = refs[len(offsets)]
-    width = refs[0].shape[1]
+def join_kernel(offsets, kept, *refs):
+    blocks, out, sems = refs[:-2], refs[-2], refs[-1]
+    width = blocks[0].shape[1]
     tm = lax.axis_index("tm")
+    stayed = lax.axis_index("segment") == lax.axis_index("head")
+    copies = []
     for at, offset in enumerate(offsets):
-        out[:, pl.ds(pl.multiple_of((tm ^ offset) * width, 128), width)] = refs[at][...]
+        target = out.at[:, pl.ds(pl.multiple_of((tm ^ offset) * width, 128), width)]
+        copy = pltpu.make_async_copy(blocks[at], target, sems.at[at])
+        copies.append(copy)
+        if offset == 0:
+            mine = pltpu.make_async_copy(kept, target, sems.at[at])
+
+            @pl.when(stayed)
+            def _():
+                mine.start()
+
+            @pl.when(jnp.logical_not(stayed))
+            def _():
+                copy.start()
+
+        else:
+            copy.start()
+    for copy in copies:
+        copy.wait()
 
 
 def grant(size):
@@ -259,7 +292,14 @@
     ids = jnp.concatenate(
         [lax.dynamic_slice_in_dim(span_ids, (tm ^ offset) * rows, rows, 0) for offset in offsets]
     )
-    ids_row, ids_column = ids.reshape(1, total), ids.reshape(total, 1)
+    bias = pl.pallas_call(
+        mask_kernel,
+        out_shape=jax.ShapeDtypeStruct((total, total), jnp.float32),
+        in_specs=[vmem, vmem],
+        out_specs=vmem,
+        compiler_params=grant(4 << 20),
+        name="mask",
+    )(ids.reshape(1, total), ids.reshape(total, 1))
 
     def pack(at, *after):
         offset = offsets[at]
@@ -285,36 +325,42 @@
 
     own, other = [], []
     for at, offset in enumerate(offsets):
-        payload = pack(at, *((ids_row, ids_column) if at == blocks - 1 else ()))
+        payload = pack(at, *((bias,) if at == blocks - 1 else ()))
         own.append(swapped(payload, offset, blocks))
     for payload in own:
         other.append(lax.ppermute(payload, "head", [(0, 1), (1, 0)]))
     results = pl.pallas_call(
         functools.partial(attend_kernel, offsets, rows),
         out_shape=[jax.ShapeDtypeStruct((rows, width), jnp.bfloat16)] * blocks,
-        in_specs=[vmem] * (2 + 2 * blocks),
+        in_specs=[vmem] * (1 + 2 * blocks),
         out_specs=[vmem] * blocks,
-        scratch_shapes=[pltpu.VMEM((total, total), jnp.float32)],
         compiler_params=grant(12 << 20),
         name="attend",
-    )(ids_row, ids_column, *own, *other)
-    back = []
-    for at, offset in enumerate(offsets):
-        back.append(swapped(results[at], offset, blocks))
+    )(bias, *own, *other)
+    back = {}
+    for offset in return_order(blocks):
+        result = results[offsets.index(offset)]
+        back[offset] = swapped(result, offset, blocks, own=False)
     joined = pl.pallas_call(
         functools.partial(join_kernel, offsets),
         out_shape=jax.ShapeDtypeStruct((rows, features), jnp.bfloat16),
-        in_specs=[vmem] * blocks,
-        out_specs=vmem,
+        in_specs=[vmem] * (1 + blocks),
+        out_specs=anywhere,
+        scratch_shapes=[pltpu.SemaphoreType.DMA((blocks,))],
         compiler_params=grant(2 << 20),
         name="join",
-    )(*back)
+    )(results[offsets.index(0)], *[back[offset] for offset in offsets])
     return joined[None]
 
 
 def send_order(blocks):
     far = blocks // 2
     return (far, *range(1, far), *range(far + 1, blocks), 0)
+
+
+def return_order(blocks):
+    far = blocks // 2
+    return (*range(far, blocks), *reversed(range(far)))
 
 
 def solution(mesh):

time: 40.6 us -> 40.4 us (level)
  Pallas kernels: 7.47 us -> 6.88 us
  starting transfers between devices: 19.6 us -> 20.1 us
    pallas_call x1, Pallas kernels: 2.39 us -> 1.62 us  [by_heads(): pl.pallas_call(functools.partial(attend_kernel, offsets, rows), out_shape...]
    ppermute x8, starting transfers between devices: 19.1 us -> 19.7 us  [swapped(): return lax.ppermute(array, MESH_TAIL, pairs)]
where the time goes in v2:
time: 40.4 us; the launch traced here: 40.1 us
  starting transfers between devices  20.1 us (50%)
  waiting for transfers between devices  12 us (30%)
  Pallas kernels  6.88 us (17%)
  local copies, waits for them, and re-layouts  0.87 us (2%)
    ppermute x8, starting transfers between devices, swapped(): return lax.ppermute(array, MESH_TAIL, pairs)  19.7 us
    ppermute x8, waiting for transfers between devices, swapped(): return lax.ppermute(array, MESH_TAIL, pairs)  10.6 us
    pallas_call x4, Pallas kernels, pack(): pl.pallas_call(functools.partial(pack_kernel, offset), out_shape=jax.Shap...  4.32 us
    pallas_call x1, Pallas kernels, by_heads(): pl.pallas_call(functools.partial(attend_kernel, offsets, rows), out_shape...  1.62 us
    ppermute x4, waiting for transfers between devices, by_heads(): other.append(lax.ppermute(payload, 'head', [(0, 1), (1, 0)]))  1.42 us
  transfers between devices with their start and end apart: 12, of which 6 were waited for; matrix products, arithmetic and copies ran while one was open for 0% of the time, Pallas kernels for 8%

profile of v2, /device:TPU:1, one launch (start us, length us, event | category | flops | bytes accessed | tf_op | source)
XLA Modules:
  0.0 40.1 jit_solution(9772606782250985418)
XLA Ops:
  0.0 0.7 %copy-done = s32[384]{0:T(512)S(1)} copy-done((s32[384]{0:T(512)S(1)}, s32[384]{0:T(512)}, u32[]{:S(2)}) %copy-start) | copy-done | bytes 1560
  0.7 0.1 fusion
  0.8 0.1 pad_add_fusion
  0.9 0.1 reshape.8.query_ids
  1.0 0.2 mask.1.refs_2_.refs_0_
  1.2 1.1 %shard_map.76 = bf16[256,384]{1,0:T(8,128)(2,1)S(1)} custom-call(bf16[96,1536]{1,0:T(8,128)(2,1)} %bitcast.3, bf16[96,1536]{1,0:T(8,128)(2,1)} %bitcast.7, bf16[96,1536]{1,0:T(8,128)(2,1)} %hidden_hbm.7, f32[1,128]{1,0:T(1,128)} %kgain_hbm.7, f32[1,128]{1,0:T(1,128)} %refs_0_.1, f32[1,1536]{1,0:T(1,128)} %refs_1_.1, f32[384,384]{1,0:T(8,128)S(1)} %mask.1.refs_2_.refs_0_), custom_call_target="tpu_custom_call" | custom-call | tf_op jit(solution)/shard_map/pallas_call | solution.py:311
  2.3 4.5 %collective-permute-start.3 = (bf16[256,384]{1,0:T(8,128)(2,1)S(1)}, bf16[256,384]{1,0:T(8,128)(2,1)S(1)}, u32[]{:S(2)}, u32[]{:S(2)}) collective-permute-start(bf16[256,384]{1,0:T(8,128)(2,1)S(1)} %shard_map.76), channel_id=1, source_target_pairs={{0,0},{1,2},{2,1},{3,3},{4,4},{5,6},{6,5},{7,7},{8,8},{9,10},{10,9... | collective-permute-start | bytes 589832 | tf_op jit(solution)/shard_map/ppermute | solution.py:115
  6.8 1.1 %shard_map.73 = bf16[240,384]{1,0:T(8,128)(2,1)S(1)} custom-call(bf16[96,1536]{1,0:T(8,128)(2,1)} %bitcast.4, bf16[96,1536]{1,0:T(8,128)(2,1)} %bitcast.8, bf16[96,1536]{1,0:T(8,128)(2,1)} %hidden_hbm.7, f32[1,128]{1,0:T(1,128)} %kgain_hbm.7), custom_call_target="tpu_custom_call" | custom-call | tf_op jit(solution)/shard_map/pallas_call | solution.py:311
  7.9 2.1 %collective-permute-start = (bf16[240,384]{1,0:T(8,128)(2,1)S(1)}, bf16[240,384]{1,0:T(8,128)(2,1)S(1)}, u32[]{:S(2)}, u32[]{:S(2)}) collective-permute-start(bf16[240,384]{1,0:T(8,128)(2,1)S(1)} %shard_map.73), channel_id=1, source_target_pairs={{0,8},{1,10},{2,9},{3,11},{4,12},{5,14},{6,13},{7,15},{8,0},{9,2},... | collective-permute-start | bytes 552968 | tf_op jit(solution)/shard_map/ppermute | solution.py:115
  10.0 1.1 %shard_map.74 = bf16[240,384]{1,0:T(8,128)(2,1)S(1)} custom-call(bf16[96,1536]{1,0:T(8,128)(2,1)} %bitcast.5, bf16[96,1536]{1,0:T(8,128)(2,1)} %bitcast.9, bf16[96,1536]{1,0:T(8,128)(2,1)} %hidden_hbm.7, f32[1,128]{1,0:T(1,128)} %kgain_hbm.7), custom_call_target="tpu_custom_call" | custom-call | tf_op jit(solution)/shard_map/pallas_call | solution.py:311
  11.1 2.8 %collective-permute-start.1 = (bf16[240,384]{1,0:T(8,128)(2,1)S(1)}, bf16[240,384]{1,0:T(8,128)(2,1)S(1)}, u32[]{:S(2)}, u32[]{:S(2)}) collective-permute-start(bf16[240,384]{1,0:T(8,128)(2,1)S(1)} %shard_map.74), channel_id=1, source_target_pairs={{0,4},{1,6},{2,5},{3,7},{4,0},{5,2},{6,1},{7,3},{8,12},{9,14},{10,... | collective-permute-start | bytes 552968 | tf_op jit(solution)/shard_map/ppermute | solution.py:115
  13.9 1.1 %shard_map.75 = bf16[240,384]{1,0:T(8,128)(2,1)S(1)} custom-call(bf16[96,1536]{1,0:T(8,128)(2,1)} %bitcast.6, bf16[96,1536]{1,0:T(8,128)(2,1)} %bitcast.10, bf16[96,1536]{1,0:T(8,128)(2,1)} %hidden_hbm.7, f32[1,128]{1,0:T(1,128)} %kgain_hbm.7), custom_call_target="tpu_custom_call" | custom-call | tf_op jit(solution)/shard_map/pallas_call | solution.py:311
  15.1 5.5 %collective-permute-done.refs_1_ = bf16[240,384]{1,0:T(8,128)(2,1)S(1)} collective-permute-done((bf16[240,384]{1,0:T(8,128)(2,1)S(1)}, bf16[240,384]{1,0:T(8,128)(2,1)S(1)}, u32[]{:S(2)}, u32[]{:S(2)}) %collective-permute-start) | collective-permute-done | bytes 184352 | tf_op jit(solution)/shard_map/ppermute | solution.py:115
  20.7 0.1 collective-permute-done.1.refs_2_
  20.8 0.4 collective-permute-start.5
  21.2 1.6 %collective-permute-done.2.refs_3_ = bf16[240,384]{1,0:T(8,128)(2,1)S(1)} collective-permute-done((bf16[240,384]{1,0:T(8,128)(2,1)S(1)}, bf16[240,384]{1,0:T(8,128)(2,1)S(1)}, u32[]{:S(2)}, u32[]{:S(2)}) %collective-permute-start.2) | collective-permute-done | bytes 184352 | tf_op jit(solution)/shard_map/ppermute | solution.py:115
  22.8 1.4 %collective-permute-done.6.refs_7_ = bf16[240,384]{1,0:T(8,128)(2,1)S(1)} collective-permute-done((bf16[240,384]{1,0:T(8,128)(2,1)S(1)}, bf16[240,384]{1,0:T(8,128)(2,1)S(1)}, u32[]{:S(2)}, u32[]{:S(2)}) %collective-permute-start.6) | collective-permute-done | bytes 184352 | tf_op jit(solution)/shard_map/ppermute | solution.py:331
  24.2 1.6 %attend.1 = (bf16[96,384]{1,0:T(8,128)(2,1)S(1)}, bf16[96,384]{1,0:T(8,128)(2,1)S(1)}, bf16[96,384]{1,0:T(8,128)(2,1)S(1)}, bf16[96,384]{1,0:T(8,128)(2,1)S(1)}) custom-call(f32[384,384]{1,0:T(8,128)S(1)} %mask.1.refs_2_.refs_0_, bf16[240,384]{1,0:T(8,128)(2,1)S(1)} %collective-permute-done.refs_1_, bf16[240,384]{1,0:T(8,128)(2,1)S(1)} %collective-permute-done.1.refs_2_, ...), custom_call_target="tpu_custom_call" | custom-call | tf_op jit(solution)/shard_map/attend/pallas_call | solution.py:332
  25.8 5.6 %collective-permute-start.8 = (bf16[96,384]{1,0:T(8,128)(2,1)S(1)}, bf16[96,384]{1,0:T(8,128)(2,1)S(1)}, u32[]{:S(2)}, u32[]{:S(2)}) collective-permute-start(bf16[96,384]{1,0:T(8,128)(2,1)S(1)} %get-tuple-element.10), channel_id=1, source_target_pairs={{0,8},{1,10},{2,9},{3,11},{4,12},{5,14},{6,13},{7,15},{8,0},{9,2},... | collective-permute-start | bytes 221192 | tf_op jit(solution)/shard_map/ppermute | solution.py:115
  31.4 1.9 %collective-permute-start.10 = (bf16[96,384]{1,0:T(8,128)(2,1)S(1)}, bf16[96,384]{1,0:T(8,128)(2,1)S(1)}, u32[]{:S(2)}, u32[]{:S(2)}) collective-permute-start(bf16[96,384]{1,0:T(8,128)(2,1)S(1)} %get-tuple-element.12), channel_id=1, source_target_pairs={{0,12},{1,14},{2,13},{3,15},{4,8},{5,10},{6,9},{7,11},{8,4},{9,6},... | collective-permute-start | bytes 221192 | tf_op jit(solution)/shard_map/ppermute | solution.py:115
  33.3 2.7 %collective-permute-start.11 = (bf16[96,384]{1,0:T(8,128)(2,1)S(1)}, bf16[96,384]{1,0:T(8,128)(2,1)S(1)}, u32[]{:S(2)}, u32[]{:S(2)}) collective-permute-start(bf16[96,384]{1,0:T(8,128)(2,1)S(1)} %get-tuple-element.9.kept), channel_id=1, source_target_pairs={{1,2},{2,1},{5,6},{6,5},{9,10},{10,9},{13,14},{14,13},{17,18},{18,... | collective-permute-start | bytes 221192 | tf_op jit(solution)/shard_map/ppermute | solution.py:115
  36.1 2.6 %collective-permute-done.9.refs_1_ = bf16[96,384]{1,0:T(8,128)(2,1)S(1)} collective-permute-done((bf16[96,384]{1,0:T(8,128)(2,1)S(1)}, bf16[96,384]{1,0:T(8,128)(2,1)S(1)}, u32[]{:S(2)}, u32[]{:S(2)}) %collective-permute-start.9) | collective-permute-done | bytes 73760 | tf_op jit(solution)/shard_map/ppermute | solution.py:115
  38.7 0.7 %collective-permute-done.11.refs_3_ = bf16[96,384]{1,0:T(8,128)(2,1)S(1)} collective-permute-done((bf16[96,384]{1,0:T(8,128)(2,1)S(1)}, bf16[96,384]{1,0:T(8,128)(2,1)S(1)}, u32[]{:S(2)}, u32[]{:S(2)}) %collective-permute-start.11) | collective-permute-done | bytes 73760 | tf_op jit(solution)/shard_map/ppermute | solution.py:115
  39.4 0.7 %join.1 = bf16[96,1536]{1,0:T(8,128)(2,1)} custom-call(bf16[96,384]{1,0:T(8,128)(2,1)S(1)} %get-tuple-element.9.kept, bf16[96,384]{1,0:T(8,128)(2,1)S(1)} %collective-permute-done.8.refs_0_, bf16[96,384]{1,0:T(8,128)(2,1)S(1)} %collective-permute-done.9.refs_1_, bf16[96,384]{1,0:T(8,128)(2,1)S(1)} %collective-permute-done.10.refs_2_, ...), custom_call_target="tpu_custom_call" | custom-call | tf_op jit(solution)/shard_map/join/pallas_call | solution.py:344
  (13 shorter events, 0.2 us)
Async XLA Ops:
  0.0 0.7 %copy-start = (s32[384]{0:T(512)S(1)}, s32[384]{0:T(512)}, u32[]{:S(2)}) copy-start(s32[384]{0:T(512)} %param.13) | copy-start | bytes 4612
  2.3 12.7 %collective-permute-start.3 = (bf16[256,384]{1,0:T(8,128)(2,1)S(1)}, bf16[256,384]{1,0:T(8,128)(2,1)S(1)}, u32[]{:S(2)}, u32[]{:S(2)}) collective-permute-start(bf16[256,384]{1,0:T(8,128)(2,1)S(1)} %shard_map.76), channel_id=1, source_target_pairs={{0,0},{1,2},{2,1},{3,3},{4,4},{5,6},{6,5},{7,7},{8,8},{9,10},{10,9... | collective-permute-start | bytes 589832 | tf_op jit(solution)/shard_map/ppermute | solution.py:115
  7.9 12.8 %collective-permute-start = (bf16[240,384]{1,0:T(8,128)(2,1)S(1)}, bf16[240,384]{1,0:T(8,128)(2,1)S(1)}, u32[]{:S(2)}, u32[]{:S(2)}) collective-permute-start(bf16[240,384]{1,0:T(8,128)(2,1)S(1)} %shard_map.73), channel_id=1, source_target_pairs={{0,8},{1,10},{2,9},{3,11},{4,12},{5,14},{6,13},{7,15},{8,0},{9,2},... | collective-permute-start | bytes 552968 | tf_op jit(solution)/shard_map/ppermute | solution.py:115
  11.1 9.7 %collective-permute-start.1 = (bf16[240,384]{1,0:T(8,128)(2,1)S(1)}, bf16[240,384]{1,0:T(8,128)(2,1)S(1)}, u32[]{:S(2)}, u32[]{:S(2)}) collective-permute-start(bf16[240,384]{1,0:T(8,128)(2,1)S(1)} %shard_map.74), channel_id=1, source_target_pairs={{0,4},{1,6},{2,5},{3,7},{4,0},{5,2},{6,1},{7,3},{8,12},{9,14},{10,... | collective-permute-start | bytes 552968 | tf_op jit(solution)/shard_map/ppermute | solution.py:115
  14.9 7.8 %collective-permute-start.2 = (bf16[240,384]{1,0:T(8,128)(2,1)S(1)}, bf16[240,384]{1,0:T(8,128)(2,1)S(1)}, u32[]{:S(2)}, u32[]{:S(2)}) collective-permute-start(bf16[240,384]{1,0:T(8,128)(2,1)S(1)} %shard_map.75), channel_id=1, source_target_pairs={{0,12},{1,14},{2,13},{3,15},{4,8},{5,10},{6,9},{7,11},{8,4},{9,6},... | collective-permute-start | bytes 552968 | tf_op jit(solution)/shard_map/ppermute | solution.py:115
  15.0 9.2 %collective-permute-start.7 = (bf16[256,384]{1,0:T(8,128)(2,1)S(1)}, bf16[256,384]{1,0:T(8,128)(2,1)S(1)}, u32[]{:S(2)}, u32[]{:S(2)}) collective-permute-start(bf16[256,384]{1,0:T(8,128)(2,1)S(1)} %collective-permute-done.3.refs_4_), channel_id=1, source_target_pairs={{0,1},{1,0},{2,3},{3,2},{4,5},{5,4},{6,7},{7,6},{8,9},{9,8},{10,11... | collective-permute-start | bytes 589832 | tf_op jit(solution)/shard_map/ppermute | solution.py:331
  20.6 2.1 %collective-permute-start.4 = (bf16[240,384]{1,0:T(8,128)(2,1)S(1)}, bf16[240,384]{1,0:T(8,128)(2,1)S(1)}, u32[]{:S(2)}, u32[]{:S(2)}) collective-permute-start(bf16[240,384]{1,0:T(8,128)(2,1)S(1)} %collective-permute-done.refs_1_), channel_id=1, source_target_pairs={{0,1},{1,0},{2,3},{3,2},{4,5},{5,4},{6,7},{7,6},{8,9},{9,8},{10,11... | collective-permute-start | bytes 552968 | tf_op jit(solution)/shard_map/ppermute | solution.py:331
  20.8 2.0 %collective-permute-start.5 = (bf16[240,384]{1,0:T(8,128)(2,1)S(1)}, bf16[240,384]{1,0:T(8,128)(2,1)S(1)}, u32[]{:S(2)}, u32[]{:S(2)}) collective-permute-start(bf16[240,384]{1,0:T(8,128)(2,1)S(1)} %collective-permute-done.1.refs_2_), channel_id=1, source_target_pairs={{0,1},{1,0},{2,3},{3,2},{4,5},{5,4},{6,7},{7,6},{8,9},{9,8},{10,11... | collective-permute-start | bytes 552968 | tf_op jit(solution)/shard_map/ppermute | solution.py:331
  22.8 1.4 %collective-permute-start.6 = (bf16[240,384]{1,0:T(8,128)(2,1)S(1)}, bf16[240,384]{1,0:T(8,128)(2,1)S(1)}, u32[]{:S(2)}, u32[]{:S(2)}) collective-permute-start(bf16[240,384]{1,0:T(8,128)(2,1)S(1)} %collective-permute-done.2.refs_3_), channel_id=1, source_target_pairs={{0,1},{1,0},{2,3},{3,2},{4,5},{5,4},{6,7},{7,6},{8,9},{9,8},{10,11... | collective-permute-start | bytes 552968 | tf_op jit(solution)/shard_map/ppermute | solution.py:331
  25.8 10.2 %collective-permute-start.8 = (bf16[96,384]{1,0:T(8,128)(2,1)S(1)}, bf16[96,384]{1,0:T(8,128)(2,1)S(1)}, u32[]{:S(2)}, u32[]{:S(2)}) collective-permute-start(bf16[96,384]{1,0:T(8,128)(2,1)S(1)} %get-tuple-element.10), channel_id=1, source_target_pairs={{0,8},{1,10},{2,9},{3,11},{4,12},{5,14},{6,13},{7,15},{8,0},{9,2},... | collective-permute-start | bytes 221192 | tf_op jit(solution)/shard_map/ppermute | solution.py:115
  31.4 7.3 %collective-permute-start.9 = (bf16[96,384]{1,0:T(8,128)(2,1)S(1)}, bf16[96,384]{1,0:T(8,128)(2,1)S(1)}, u32[]{:S(2)}, u32[]{:S(2)}) collective-permute-start(bf16[96,384]{1,0:T(8,128)(2,1)S(1)} %get-tuple-element.11), channel_id=1, source_target_pairs={{0,4},{1,6},{2,5},{3,7},{4,0},{5,2},{6,1},{7,3},{8,12},{9,14},{10,... | collective-permute-start | bytes 221192 | tf_op jit(solution)/shard_map/ppermute | solution.py:115
  31.4 7.3 %collective-permute-start.10 = (bf16[96,384]{1,0:T(8,128)(2,1)S(1)}, bf16[96,384]{1,0:T(8,128)(2,1)S(1)}, u32[]{:S(2)}, u32[]{:S(2)}) collective-permute-start(bf16[96,384]{1,0:T(8,128)(2,1)S(1)} %get-tuple-element.12), channel_id=1, source_target_pairs={{0,12},{1,14},{2,13},{3,15},{4,8},{5,10},{6,9},{7,11},{8,4},{9,6},... | collective-permute-start | bytes 221192 | tf_op jit(solution)/shard_map/ppermute | solution.py:115
  33.3 6.0 %collective-permute-start.11 = (bf16[96,384]{1,0:T(8,128)(2,1)S(1)}, bf16[96,384]{1,0:T(8,128)(2,1)S(1)}, u32[]{:S(2)}, u32[]{:S(2)}) collective-permute-start(bf16[96,384]{1,0:T(8,128)(2,1)S(1)} %get-tuple-element.9.kept), channel_id=1, source_target_pairs={{1,2},{2,1},{5,6},{6,5},{9,10},{10,9},{13,14},{14,13},{17,18},{18,... | collective-permute-start | bytes 221192 | tf_op jit(solution)/shard_map/ppermute | solution.py:115

commit v3 on v2

--- a/solution.py
+++ b/solution.py
@@ -129,43 +129,53 @@
     return [part.astype(jnp.float32) for part in (high, middle, low)]
 
 
-def pack_kernel(offset, key_hbm, value_hbm, hidden_hbm, kgain_hbm, *refs):
-    out, kgain, qgain, gate, sems = refs[-5:]
+def pack_kernel(pieces, width, key_hbm, value_hbm, hidden_hbm, qgain_hbm, kgain_hbm, gate_hbm, *refs):
+    outs, (kgain, qgain, gate, sems) = refs[: len(pieces)], refs[len(pieces) :]
     rows = key_hbm.shape[0]
-    width = out.shape[1]
     half = rows // 2
     tm = lax.axis_index("tm")
     first = pl.multiple_of(lax.axis_index("segment") * half, 16)
-    columns = pl.ds(pl.multiple_of((tm ^ offset) * width, 128), width)
-    moves = [
-        (key_hbm.at[:, columns], out.at[pl.ds(0, rows)]),
-        (kgain_hbm, kgain),
-        (value_hbm.at[:, columns], out.at[pl.ds(rows, rows)]),
-        (hidden_hbm.at[pl.ds(first, half), columns], out.at[pl.ds(2 * rows, half)]),
-    ]
-    if offset == 0:
-        moves += [(refs[0], qgain), (refs[1].at[:, columns], gate)]
+    taken = 0
+
+    def start(source, target):
+        nonlocal taken
+        copy = pltpu.make_async_copy(source, target, sems.at[taken])
+        taken += 1
+        copy.start()
+        return copy
+
     copies = []
-    for which, (source, target) in enumerate(moves):
-        copy = pltpu.make_async_copy(source, target, sems.at[which])
-        copy.start()
-        copies.append(copy)
-    copies[0].wait()
-    copies[1].wait()
-    gain = kgain[...]
-    for head in range(width // HEAD_DIM):
-        lanes = pl.ds(head * HEAD_DIM, HEAD_DIM)
-        out[pl.ds(0, rows), lanes] = normed(out[pl.ds(0, rows), lanes], gain)
-    for copy in copies[2:]:
-        copy.wait()
-    if offset == 0:
-        query_row = jnp.concatenate([qgain[...]] * (width // HEAD_DIM), axis=1)
-        parts = split_parts(gate[...]) + split_parts(query_row)
-        index = lax.broadcasted_iota(jnp.int32, (PART_ROWS, width), 0)
-        table = jnp.zeros((PART_ROWS, width), jnp.float32)
-        for line, part in enumerate(parts):
-            table = jnp.where(index == line, part, table)
-        out[pl.ds(2 * rows + half, PART_ROWS), :] = table.astype(jnp.bfloat16)
+    for out, (offset, head) in zip(outs, pieces):
+        base = (tm ^ offset) * width + head * HEAD_DIM
+        columns = pl.ds(pl.multiple_of(base, 128), out.shape[1])
+        row = [start(key_hbm.at[:, columns], out.at[pl.ds(0, rows)])]
+        if not copies:
+            row.append(start(kgain_hbm, kgain))
+        row += [
+            start(value_hbm.at[:, columns], out.at[pl.ds(rows, rows)]),
+            start(hidden_hbm.at[pl.ds(first, half), columns], out.at[pl.ds(2 * rows, half)]),
+        ]
+        if offset == 0:
+            row += [start(qgain_hbm, qgain), start(gate_hbm.at[:, columns], gate)]
+        copies.append(row)
+    for at, (out, (offset, _)) in enumerate(zip(outs, pieces)):
+        copies[at][0].wait()
+        if at == 0:
+            copies[at].pop(1).wait()
+        gain = kgain[...]
+        for head in range(out.shape[1] // HEAD_DIM):
+            lanes = pl.ds(head * HEAD_DIM, HEAD_DIM)
+            out[pl.ds(0, rows), lanes] = normed(out[pl.ds(0, rows), lanes], gain)
+        for copy in copies[at][1:]:
+            copy.wait()
+        if offset == 0:
+            query_row = jnp.concatenate([qgain[...]] * (width // HEAD_DIM), axis=1)
+            parts = split_parts(gate[...]) + split_parts(query_row)
+            index = lax.broadcasted_iota(jnp.int32, (PART_ROWS, width), 0)
+            table = jnp.zeros((PART_ROWS, width), jnp.float32)
+            for line, part in enumerate(parts):
+                table = jnp.where(index == line, part, table)
+            out[pl.ds(2 * rows + half, PART_ROWS), :] = table.astype(jnp.bfloat16)
 
 
 def mask_kernel(key_ids, query_ids, bias):
@@ -187,53 +197,55 @@
     return (current.astype(jnp.float32) + gate * mixture).astype(jnp.bfloat16)
 
 
-def attend_kernel(offsets, rows, *refs):
+def attend_kernel(offsets, rows, heads, bases, *refs):
     count = len(offsets)
-    bias_ref, refs = refs[0], refs[1:]
-    own, other, outs = refs[:count], refs[count : 2 * count], refs[2 * count : 3 * count]
-    width = outs[0].shape[1]
+    bias_ref, own, other, outs = refs[0], refs[1 : 1 + count], refs[1 + count : 1 + 2 * count], refs[-count:]
     half = rows // 2
 
     def run(first, second, last):
-        def part(refs_, start, size, lanes):
-            return jnp.concatenate([ref[pl.ds(start, size), lanes] for ref in refs_], axis=0)
-
-        def table(refs_, line, lanes):
-            block = refs_[offsets.index(0)][pl.ds(2 * rows + half, PART_ROWS), lanes]
+        def lanes(at, head):
+            return pl.ds((head - bases[at]) * HEAD_DIM, HEAD_DIM)
+
+        def part(source, start, head):
+            return jnp.concatenate(
+                [ref[pl.ds(start, rows), lanes(at, head)] for at, ref in enumerate(source)], axis=0
+            )
+
+        def table(source, line, head):
+            at = offsets.index(0)
+            block = source[at][pl.ds(2 * rows + half, PART_ROWS), lanes(at, head)]
             block = block.astype(jnp.float32)
             return block[line : line + 1] + (
                 block[line + 1 : line + 2] + block[line + 2 : line + 3]
             )
 
-        heads = range(width // HEAD_DIM)
-        lanes_of = [pl.ds(head * HEAD_DIM, HEAD_DIM) for head in heads]
-        current = [
-            jnp.concatenate(
+        current = {
+            head: jnp.concatenate(
                 [
-                    ref[pl.ds(2 * rows, half), lanes]
+                    ref[pl.ds(2 * rows, half), lanes(at, head)]
                     for at in range(count)
                     for ref in (first[at], second[at])
                 ],
                 axis=0,
             )
-            for lanes in lanes_of
-        ]
+            for head in heads
+        }
         bias = bias_ref[...]
         for section in range(last + 1):
             source = (first, second)[section]
             for head in heads:
-                lanes = lanes_of[head]
                 current[head] = layer_rows(
                     current[head],
-                    part(source, 0, rows, lanes),
-                    part(source, rows, rows, lanes),
+                    part(source, 0, head),
+                    part(source, rows, head),
                     bias,
-                    table(source, 3, lanes),
-                    table(source, 0, lanes),
+                    table(source, 3, head),
+                    table(source, 0, head),
                 )
         for head in heads:
+            columns = pl.ds(head * HEAD_DIM, HEAD_DIM)
             for at in range(count):
-                outs[at][:, lanes_of[head]] = current[head][at * rows : (at + 1) * rows]
+                outs[at][:, columns] = current[head][at * rows : (at + 1) * rows]
 
     core = lax.axis_index("head")
 
@@ -284,10 +296,50 @@
     half = rows // 2
     total = rows * blocks
     tm = lax.axis_index("tm")
-    offsets = send_order(blocks)
     vmem = pl.BlockSpec(memory_space=pltpu.VMEM)
     hbm = pl.BlockSpec(memory_space=pltpu.HBM)
     anywhere = pl.BlockSpec(memory_space=pl.ANY)
+
+    count = width // HEAD_DIM
+    groups = [(0, count - 1), (count - 1, 1)] if count > 1 else [(0, 1)]
+    sends = send_order(blocks, len(groups))
+    offsets = tuple(dict.fromkeys(offset for offset, _ in sends))
+    late = sends[-1][0]
+
+    sources = [key_cache[0], value_cache[0], hidden_in, query_gain, key_gain, out_gate]
+    sources = [pltpu.with_memory_space_constraint(source, pltpu.HBM) for source in sources]
+
+    def pack(chosen):
+        shapes = [
+            jax.ShapeDtypeStruct(
+                (
+                    2 * rows + half + (PART_ROWS if offset == 0 else 0),
+                    groups[piece][1] * HEAD_DIM if offset == late else width,
+                ),
+                jnp.bfloat16,
+            )
+            for offset, piece in chosen
+        ]
+        heads = [(offset, groups[piece][0] if offset == late else 0) for offset, piece in chosen]
+        return pl.pallas_call(
+            functools.partial(pack_kernel, tuple(heads), width),
+            out_shape=shapes,
+            in_specs=[hbm] * len(sources),
+            out_specs=[vmem] * len(shapes),
+            scratch_shapes=[
+                pltpu.VMEM((1, HEAD_DIM), jnp.float32),
+                pltpu.VMEM((1, HEAD_DIM), jnp.float32),
+                pltpu.VMEM((1, width), jnp.float32),
+                pltpu.SemaphoreType.DMA((3 * len(shapes) + 3,)),
+            ],
+            compiler_params=grant(4 << 20),
+        )(*sources)
+
+    payloads = [*pack(sends[:1]), *pack(sends[1:])]
+    own, other = {}, {}
+    for key, payload in zip(sends, payloads):
+        own[key] = swapped(payload, key[0], blocks)
+        other[key] = lax.ppermute(own[key], "head", [(0, 1), (1, 0)])
 
     ids = jnp.concatenate(
         [lax.dynamic_slice_in_dim(span_ids, (tm ^ offset) * rows, rows, 0) for offset in offsets]
@@ -301,42 +353,21 @@
         name="mask",
     )(ids.reshape(1, total), ids.reshape(total, 1))
 
-    def pack(at, *after):
-        offset = offsets[at]
-        size = 2 * rows + half + (PART_ROWS if offset == 0 else 0)
-        sources = [key_cache[0], value_cache[0], hidden_in, key_gain]
-        if offset == 0:
-            sources += [query_gain, out_gate]
-        sources = [pltpu.with_memory_space_constraint(source, pltpu.HBM) for source in sources]
-        payload = pl.pallas_call(
-            functools.partial(pack_kernel, offset),
-            out_shape=jax.ShapeDtypeStruct((size, width), jnp.bfloat16),
-            in_specs=[hbm] * len(sources) + [anywhere] * len(after),
-            out_specs=vmem,
-            scratch_shapes=[
-                pltpu.VMEM((1, HEAD_DIM), jnp.float32),
-                pltpu.VMEM((1, HEAD_DIM), jnp.float32),
-                pltpu.VMEM((1, width), jnp.float32),
-                pltpu.SemaphoreType.DMA((6,)),
-            ],
-            compiler_params=grant(2 << 20),
-        )(*sources, *after)
-        return payload
-
-    own, other = [], []
-    for at, offset in enumerate(offsets):
-        payload = pack(at, *((bias,) if at == blocks - 1 else ()))
-        own.append(swapped(payload, offset, blocks))
-    for payload in own:
-        other.append(lax.ppermute(payload, "head", [(0, 1), (1, 0)]))
-    results = pl.pallas_call(
-        functools.partial(attend_kernel, offsets, rows),
-        out_shape=[jax.ShapeDtypeStruct((rows, width), jnp.bfloat16)] * blocks,
-        in_specs=[vmem] * (1 + 2 * blocks),
-        out_specs=[vmem] * blocks,
-        compiler_params=grant(12 << 20),
-        name="attend",
-    )(bias, *own, *other)
+    results = []
+    for group, (start, heads) in enumerate(groups):
+        chosen = [(offset, group if offset == late else 0) for offset in offsets]
+        bases = tuple(start if offset == late else 0 for offset in offsets)
+        operands = [bias, *[own[key] for key in chosen], *[other[key] for key in chosen], *results]
+        results = pl.pallas_call(
+            functools.partial(
+                attend_kernel, offsets, rows, tuple(range(start, start + heads)), bases
+            ),
+            out_shape=[jax.ShapeDtypeStruct((rows, width), jnp.bfloat16)] * blocks,
+            in_specs=[vmem] * len(operands),
+            out_specs=[vmem] * blocks,
+            input_output_aliases={1 + 2 * blocks + at: at for at in range(len(results))},
+            compiler_params=grant(8 << 20),
+        )(*operands)
     back = {}
     for offset in return_order(blocks):
         result = results[offsets.index(offset)]
@@ -353,9 +384,12 @@
     return joined[None]
 
 
-def send_order(blocks):
+def send_order(blocks, pieces):
     far = blocks // 2
-    return (far, *range(1, far), *range(far + 1, blocks), 0)
+    late = blocks - 1
+    whole = [offset for offset in (far, *range(1, far), *range(far + 1, blocks)) if offset != late]
+    split = [(late, piece) for piece in range(pieces)]
+    return (*[(offset, 0) for offset in whole], *split[:-1], (0, 0), split[-1])
 
 
 def return_order(blocks):

time: 40.4 us -> 39.4 us (0.975)
  starting transfers between devices: 20.1 us -> 24 us
  waiting for transfers between devices: 12 us -> 9.17 us
  Pallas kernels: 6.88 us -> 5.56 us
  local copies, waits for them, and re-layouts: 0.87 us -> 0.19 us
    ppermute x8 -> x9, starting transfers between devices: 19.7 us -> 23 us  [swapped(): return lax.ppermute(array, MESH_TAIL, pairs)]
    ppermute x8 -> x9, waiting for transfers between devices: 10.6 us -> 8.75 us  [swapped(): return lax.ppermute(array, MESH_TAIL, pairs)]
    pallas_call x5 -> x4, Pallas kernels: 5.95 us -> 4.62 us  [the longest x2 2.61 us: pack(): pl.pallas_call(functools.partial(pack_kernel, tuple(heads), width), out_s...]
    ppermute x4 -> x5, waiting for transfers between devices: 1.42 us -> 0.43 us  [by_heads(): other[key] = lax.ppermute(own[key], 'head', [(0, 1), (1, 0)])]
    unnamed x2, local copies, waits for them, and re-layouts: 0.68 us -> 0.01 us
    ppermute x4 -> x5, starting transfers between devices: 0.45 us -> 1.04 us  [by_heads(): other[key] = lax.ppermute(own[key], 'head', [(0, 1), (1, 0)])]
  transfers between devices with their start and end apart: 12 -> 14, of which waited for: 6 -> 6; matrix products, arithmetic and copies ran while one was open for 0% -> 1% of each run, Pallas kernels for 8% -> 6%
where the time goes in v3:
time: 39.4 us; the launch traced here: 39.1 us
  starting transfers between devices  24 us (61%)
  waiting for transfers between devices  9.17 us (23%)
  Pallas kernels  5.56 us (14%)
    ppermute x9, starting transfers between devices, swapped(): return lax.ppermute(array, MESH_TAIL, pairs)  23 us
    ppermute x9, waiting for transfers between devices, swapped(): return lax.ppermute(array, MESH_TAIL, pairs)  8.75 us
    pallas_call x2, Pallas kernels, pack(): pl.pallas_call(functools.partial(pack_kernel, tuple(heads), width), out_s...  2.61 us
    pallas_call x2, Pallas kernels, by_heads(): pl.pallas_call(functools.partial(attend_kernel, offsets, rows, tuple(rang...  2.01 us
    ppermute x5, starting transfers between devices, by_heads(): other[key] = lax.ppermute(own[key], 'head', [(0, 1), (1, 0)])  1.04 us
  transfers between devices with their start and end apart: 14, of which 6 were waited for; matrix products, arithmetic and copies ran while one was open for 1% of the time, Pallas kernels for 6%

profile of v3, /device:TPU:1, one launch (start us, length us, event | category | flops | bytes accessed | tf_op | source)
XLA Modules:
  0.0 39.1 jit_solution(15238369930242650573)
XLA Ops:
  0.0 1.5 %shard_map.74 = (bf16[240,384]{1,0:T(8,128)(2,1)S(1)}, bf16[240,256]{1,0:T(8,128)(2,1)S(1)}, bf16[256,384]{1,0:T(8,128)(2,1)S(1)}, bf16[240,128]{1,0:T(8,128)(2,1)S(1)}) custom-call(bf16[96,1536]{1,0:T(8,128)(2,1)} %bitcast.3, bf16[96,1536]{1,0:T(8,128)(2,1)} %bitcast.5, bf16[96,1536]{1,0:T(8,128)(2,1)} %hidden_hbm.3, f32[1,128]{1,0:T(1,128)} %qgain_hbm.3, ...), custom_call_target="tpu_custom_call" | custom-call | tf_op jit(solution)/shard_map/pallas_call | solution.py:324
  1.5 4.5 %collective-permute-start.3 = (bf16[256,384]{1,0:T(8,128)(2,1)S(1)}, bf16[256,384]{1,0:T(8,128)(2,1)S(1)}, u32[]{:S(2)}, u32[]{:S(2)}) collective-permute-start(bf16[256,384]{1,0:T(8,128)(2,1)S(1)} %get-tuple-element.19), channel_id=1, source_target_pairs={{0,0},{1,2},{2,1},{3,3},{4,4},{5,6},{6,5},{7,7},{8,8},{9,10},{10,9... | collective-permute-start | bytes 589832 | tf_op jit(solution)/shard_map/ppermute | solution.py:115
  6.0 1.1 %shard_map.73 = bf16[240,384]{1,0:T(8,128)(2,1)S(1)} custom-call(bf16[96,1536]{1,0:T(8,128)(2,1)} %bitcast.4, bf16[96,1536]{1,0:T(8,128)(2,1)} %bitcast.6, bf16[96,1536]{1,0:T(8,128)(2,1)} %hidden_hbm.3, f32[1,128]{1,0:T(1,128)} %qgain_hbm.3, f32[1,128]{1,0:T(1,128)} %kgain_hbm.3, f32[1,1536]{1,0:T(1,128)} %gate_hbm.3), custom_call_target="tpu_custom_call" | custom-call | tf_op jit(solution)/shard_map/pallas_call | solution.py:324
  7.1 2.1 %collective-permute-start = (bf16[240,384]{1,0:T(8,128)(2,1)S(1)}, bf16[240,384]{1,0:T(8,128)(2,1)S(1)}, u32[]{:S(2)}, u32[]{:S(2)}) collective-permute-start(bf16[240,384]{1,0:T(8,128)(2,1)S(1)} %shard_map.73), channel_id=1, source_target_pairs={{0,8},{1,10},{2,9},{3,11},{4,12},{5,14},{6,13},{7,15},{8,0},{9,2},... | collective-permute-start | bytes 552968 | tf_op jit(solution)/shard_map/ppermute | solution.py:115
  9.2 2.7 %collective-permute-start.1 = (bf16[240,384]{1,0:T(8,128)(2,1)S(1)}, bf16[240,384]{1,0:T(8,128)(2,1)S(1)}, u32[]{:S(2)}, u32[]{:S(2)}) collective-permute-start(bf16[240,384]{1,0:T(8,128)(2,1)S(1)} %get-tuple-element.17), channel_id=1, source_target_pairs={{0,4},{1,6},{2,5},{3,7},{4,0},{5,2},{6,1},{7,3},{8,12},{9,14},{10,... | collective-permute-start | bytes 552968 | tf_op jit(solution)/shard_map/ppermute | solution.py:115
  12.0 4.4 %collective-permute-start.2 = (bf16[240,128]{1,0:T(8,128)(2,1)S(1)}, bf16[240,128]{1,0:T(8,128)(2,1)S(1)}, u32[]{:S(2)}, u32[]{:S(2)}) collective-permute-start(bf16[240,128]{1,0:T(8,128)(2,1)S(1)} %get-tuple-element.18), channel_id=1, source_target_pairs={{0,12},{1,14},{2,13},{3,15},{4,8},{5,10},{6,9},{7,11},{8,4},{9,6},... | collective-permute-start | bytes 184328 | tf_op jit(solution)/shard_map/ppermute | solution.py:115
  16.4 4.4 %collective-permute-done.8.refs_3_ = bf16[240,256]{1,0:T(8,128)(2,1)S(1)} collective-permute-done((bf16[240,256]{1,0:T(8,128)(2,1)S(1)}, bf16[240,256]{1,0:T(8,128)(2,1)S(1)}, u32[]{:S(2)}, u32[]{:S(2)}) %collective-permute-start.8) | collective-permute-done | bytes 122912 | tf_op jit(solution)/shard_map/ppermute | solution.py:115
  20.9 1.0 %collective-permute-done.refs_1_ = bf16[240,384]{1,0:T(8,128)(2,1)S(1)} collective-permute-done((bf16[240,384]{1,0:T(8,128)(2,1)S(1)}, bf16[240,384]{1,0:T(8,128)(2,1)S(1)}, u32[]{:S(2)}, u32[]{:S(2)}) %collective-permute-start) | collective-permute-done | bytes 184352 | tf_op jit(solution)/shard_map/ppermute | solution.py:115
  21.9 0.5 %collective-permute-start.5 = (bf16[240,384]{1,0:T(8,128)(2,1)S(1)}, bf16[240,384]{1,0:T(8,128)(2,1)S(1)}, u32[]{:S(2)}, u32[]{:S(2)}) collective-permute-start(bf16[240,384]{1,0:T(8,128)(2,1)S(1)} %collective-permute-done.1.refs_2_), channel_id=1, source_target_pairs={{0,1},{1,0},{2,3},{3,2},{4,5},{5,4},{6,7},{7,6},{8,9},{9,8},{10,11... | collective-permute-start | bytes 552968 | tf_op jit(solution)/shard_map/ppermute | solution.py:342
  22.5 0.1 fusion
  22.6 0.5 %collective-permute-start.6 = (bf16[240,128]{1,0:T(8,128)(2,1)S(1)}, bf16[240,128]{1,0:T(8,128)(2,1)S(1)}, u32[]{:S(2)}, u32[]{:S(2)}) collective-permute-start(bf16[240,128]{1,0:T(8,128)(2,1)S(1)} %collective-permute-done.2.refs_3_), channel_id=1, source_target_pairs={{0,1},{1,0},{2,3},{3,2},{4,5},{5,4},{6,7},{7,6},{8,9},{9,8},{10,11... | collective-permute-start | bytes 184328 | tf_op jit(solution)/shard_map/ppermute | solution.py:342
  23.1 0.1 reshape.8.query_ids
  23.2 0.2 mask.1.refs_0_
  23.4 0.1 collective-permute-done.5.refs_6_
  23.6 0.3 collective-permute-done.7.refs_8_
  23.9 1.1 %shard_map.75 = (bf16[96,384]{1,0:T(8,128)(2,1)S(1)}, bf16[96,384]{1,0:T(8,128)(2,1)S(1)}, bf16[96,384]{1,0:T(8,128)(2,1)S(1)}, bf16[96,384]{1,0:T(8,128)(2,1)S(1)}) custom-call(f32[384,384]{1,0:T(8,128)S(1)} %mask.1.refs_0_, bf16[240,384]{1,0:T(8,128)(2,1)S(1)} %collective-permute-done.refs_1_, bf16[240,384]{1,0:T(8,128)(2,1)S(1)} %collective-permute-done.1.refs_2_, ...), custom_call_target="tpu_custom_call" | custom-call | tf_op jit(solution)/shard_map/pallas_call | solution.py:361
  25.0 0.9 %shard_map.76 = (bf16[96,384]{1,0:T(8,128)(2,1)S(1)}, bf16[96,384]{1,0:T(8,128)(2,1)S(1)}, bf16[96,384]{1,0:T(8,128)(2,1)S(1)}, bf16[96,384]{1,0:T(8,128)(2,1)S(1)}) custom-call(f32[384,384]{1,0:T(8,128)S(1)} %mask.1.refs_0_, ...), custom_call_target="tpu_custom_call", output_to_operand_aliasing={{0}: (9, {}), {1}: (10, {}), {2}: (11, {}), {3}: (12, {})} | custom-call | tf_op jit(solution)/shard_map/pallas_call | solution.py:361
  25.9 4.6 %collective-permute-start.10 = (bf16[96,384]{1,0:T(8,128)(2,1)S(1)}, bf16[96,384]{1,0:T(8,128)(2,1)S(1)}, u32[]{:S(2)}, u32[]{:S(2)}) collective-permute-start(bf16[96,384]{1,0:T(8,128)(2,1)S(1)} %get-tuple-element.26), channel_id=1, source_target_pairs={{0,8},{1,10},{2,9},{3,11},{4,12},{5,14},{6,13},{7,15},{8,0},{9,2},... | collective-permute-start | bytes 221192 | tf_op jit(solution)/shard_map/ppermute | solution.py:115
  30.5 0.2 collective-permute-start.11
  30.7 2.0 %collective-permute-start.12 = (bf16[96,384]{1,0:T(8,128)(2,1)S(1)}, bf16[96,384]{1,0:T(8,128)(2,1)S(1)}, u32[]{:S(2)}, u32[]{:S(2)}) collective-permute-start(bf16[96,384]{1,0:T(8,128)(2,1)S(1)} %get-tuple-element.28), channel_id=1, source_target_pairs={{0,12},{1,14},{2,13},{3,15},{4,8},{5,10},{6,9},{7,11},{8,4},{9,6},... | collective-permute-start | bytes 221192 | tf_op jit(solution)/shard_map/ppermute | solution.py:115
  32.7 2.5 %collective-permute-start.13 = (bf16[96,384]{1,0:T(8,128)(2,1)S(1)}, bf16[96,384]{1,0:T(8,128)(2,1)S(1)}, u32[]{:S(2)}, u32[]{:S(2)}) collective-permute-start(bf16[96,384]{1,0:T(8,128)(2,1)S(1)} %get-tuple-element.25.kept), channel_id=1, source_target_pairs={{1,2},{2,1},{5,6},{6,5},{9,10},{10,9},{13,14},{14,13},{17,18},{18,... | collective-permute-start | bytes 221192 | tf_op jit(solution)/shard_map/ppermute | solution.py:115
  35.1 2.5 %collective-permute-done.11.refs_1_ = bf16[96,384]{1,0:T(8,128)(2,1)S(1)} collective-permute-done((bf16[96,384]{1,0:T(8,128)(2,1)S(1)}, bf16[96,384]{1,0:T(8,128)(2,1)S(1)}, u32[]{:S(2)}, u32[]{:S(2)}) %collective-permute-start.11) | collective-permute-done | bytes 73760 | tf_op jit(solution)/shard_map/ppermute | solution.py:115
  37.6 0.8 %collective-permute-done.13.refs_3_ = bf16[96,384]{1,0:T(8,128)(2,1)S(1)} collective-permute-done((bf16[96,384]{1,0:T(8,128)(2,1)S(1)}, bf16[96,384]{1,0:T(8,128)(2,1)S(1)}, u32[]{:S(2)}, u32[]{:S(2)}) %collective-permute-start.13) | collective-permute-done | bytes 73760 | tf_op jit(solution)/shard_map/ppermute | solution.py:115
  38.4 0.7 %join.1 = bf16[96,1536]{1,0:T(8,128)(2,1)} custom-call(bf16[96,384]{1,0:T(8,128)(2,1)S(1)} %get-tuple-element.25.kept, bf16[96,384]{1,0:T(8,128)(2,1)S(1)} %collective-permute-done.10.refs_0_, bf16[96,384]{1,0:T(8,128)(2,1)S(1)} %collective-permute-done.11.refs_1_, bf16[96,384]{1,0:T(8,128)(2,1)S(1)} %collective-permute-done.12.refs_2_, ...), custom_call_target="tpu_custom_call" | custom-call | tf_op jit(solution)/shard_map/join/pallas_call | solution.py:375
  (16 shorter events, 0.2 us)
Async XLA Ops:
  1.5 20.9 %collective-permute-start.3 = (bf16[256,384]{1,0:T(8,128)(2,1)S(1)}, bf16[256,384]{1,0:T(8,128)(2,1)S(1)}, u32[]{:S(2)}, u32[]{:S(2)}) collective-permute-start(bf16[256,384]{1,0:T(8,128)(2,1)S(1)} %get-tuple-element.19), channel_id=1, source_target_pairs={{0,0},{1,2},{2,1},{3,3},{4,4},{5,6},{6,5},{7,7},{8,8},{9,10},{10,9... | collective-permute-start | bytes 589832 | tf_op jit(solution)/shard_map/ppermute | solution.py:115
  7.1 14.8 %collective-permute-start = (bf16[240,384]{1,0:T(8,128)(2,1)S(1)}, bf16[240,384]{1,0:T(8,128)(2,1)S(1)}, u32[]{:S(2)}, u32[]{:S(2)}) collective-permute-start(bf16[240,384]{1,0:T(8,128)(2,1)S(1)} %shard_map.73), channel_id=1, source_target_pairs={{0,8},{1,10},{2,9},{3,11},{4,12},{5,14},{6,13},{7,15},{8,0},{9,2},... | collective-permute-start | bytes 552968 | tf_op jit(solution)/shard_map/ppermute | solution.py:115
  9.2 12.7 %collective-permute-start.1 = (bf16[240,384]{1,0:T(8,128)(2,1)S(1)}, bf16[240,384]{1,0:T(8,128)(2,1)S(1)}, u32[]{:S(2)}, u32[]{:S(2)}) collective-permute-start(bf16[240,384]{1,0:T(8,128)(2,1)S(1)} %get-tuple-element.17), channel_id=1, source_target_pairs={{0,4},{1,6},{2,5},{3,7},{4,0},{5,2},{6,1},{7,3},{8,12},{9,14},{10,... | collective-permute-start | bytes 552968 | tf_op jit(solution)/shard_map/ppermute | solution.py:115
  12.0 8.9 %collective-permute-start.8 = (bf16[240,256]{1,0:T(8,128)(2,1)S(1)}, bf16[240,256]{1,0:T(8,128)(2,1)S(1)}, u32[]{:S(2)}, u32[]{:S(2)}) collective-permute-start(bf16[240,256]{1,0:T(8,128)(2,1)S(1)} %get-tuple-element.20), channel_id=1, source_target_pairs={{0,12},{1,14},{2,13},{3,15},{4,8},{5,10},{6,9},{7,11},{8,4},{9,6},... | collective-permute-start | bytes 368648 | tf_op jit(solution)/shard_map/ppermute | solution.py:115
  12.0 10.6 %collective-permute-start.2 = (bf16[240,128]{1,0:T(8,128)(2,1)S(1)}, bf16[240,128]{1,0:T(8,128)(2,1)S(1)}, u32[]{:S(2)}, u32[]{:S(2)}) collective-permute-start(bf16[240,128]{1,0:T(8,128)(2,1)S(1)} %get-tuple-element.18), channel_id=1, source_target_pairs={{0,12},{1,14},{2,13},{3,15},{4,8},{5,10},{6,9},{7,11},{8,4},{9,6},... | collective-permute-start | bytes 184328 | tf_op jit(solution)/shard_map/ppermute | solution.py:115
  16.4 6.1 %copy-start = (s32[384]{0:T(512)S(1)}, s32[384]{0:T(512)}, u32[]{:S(2)}) copy-start(s32[384]{0:T(512)} %param.13) | copy-start | bytes 4612
  20.9 2.6 %collective-permute-start.9 = (bf16[240,256]{1,0:T(8,128)(2,1)S(1)}, bf16[240,256]{1,0:T(8,128)(2,1)S(1)}, u32[]{:S(2)}, u32[]{:S(2)}) collective-permute-start(bf16[240,256]{1,0:T(8,128)(2,1)S(1)} %collective-permute-done.8.refs_3_), channel_id=1, source_target_pairs={{0,1},{1,0},{2,3},{3,2},{4,5},{5,4},{6,7},{7,6},{8,9},{9,8},{10,11... | collective-permute-start | bytes 368648 | tf_op jit(solution)/shard_map/ppermute | solution.py:342
  21.9 1.5 %collective-permute-start.4 = (bf16[240,384]{1,0:T(8,128)(2,1)S(1)}, bf16[240,384]{1,0:T(8,128)(2,1)S(1)}, u32[]{:S(2)}, u32[]{:S(2)}) collective-permute-start(bf16[240,384]{1,0:T(8,128)(2,1)S(1)} %collective-permute-done.refs_1_), channel_id=1, source_target_pairs={{0,1},{1,0},{2,3},{3,2},{4,5},{5,4},{6,7},{7,6},{8,9},{9,8},{10,11... | collective-permute-start | bytes 552968 | tf_op jit(solution)/shard_map/ppermute | solution.py:342
  21.9 1.7 %collective-permute-start.5 = (bf16[240,384]{1,0:T(8,128)(2,1)S(1)}, bf16[240,384]{1,0:T(8,128)(2,1)S(1)}, u32[]{:S(2)}, u32[]{:S(2)}) collective-permute-start(bf16[240,384]{1,0:T(8,128)(2,1)S(1)} %collective-permute-done.1.refs_2_), channel_id=1, source_target_pairs={{0,1},{1,0},{2,3},{3,2},{4,5},{5,4},{6,7},{7,6},{8,9},{9,8},{10,11... | collective-permute-start | bytes 552968 | tf_op jit(solution)/shard_map/ppermute | solution.py:342
  22.4 1.5 %collective-permute-start.7 = (bf16[256,384]{1,0:T(8,128)(2,1)S(1)}, bf16[256,384]{1,0:T(8,128)(2,1)S(1)}, u32[]{:S(2)}, u32[]{:S(2)}) collective-permute-start(bf16[256,384]{1,0:T(8,128)(2,1)S(1)} %collective-permute-done.3.refs_4_), channel_id=1, source_target_pairs={{0,1},{1,0},{2,3},{3,2},{4,5},{5,4},{6,7},{7,6},{8,9},{9,8},{10,11... | collective-permute-start | bytes 589832 | tf_op jit(solution)/shard_map/ppermute | solution.py:342
  22.6 2.4 %collective-permute-start.6 = (bf16[240,128]{1,0:T(8,128)(2,1)S(1)}, bf16[240,128]{1,0:T(8,128)(2,1)S(1)}, u32[]{:S(2)}, u32[]{:S(2)}) collective-permute-start(bf16[240,128]{1,0:T(8,128)(2,1)S(1)} %collective-permute-done.2.refs_3_), channel_id=1, source_target_pairs={{0,1},{1,0},{2,3},{3,2},{4,5},{5,4},{6,7},{7,6},{8,9},{9,8},{10,11... | collective-permute-start | bytes 184328 | tf_op jit(solution)/shard_map/ppermute | solution.py:342
  25.9 9.2 %collective-permute-start.10 = (bf16[96,384]{1,0:T(8,128)(2,1)S(1)}, bf16[96,384]{1,0:T(8,128)(2,1)S(1)}, u32[]{:S(2)}, u32[]{:S(2)}) collective-permute-start(bf16[96,384]{1,0:T(8,128)(2,1)S(1)} %get-tuple-element.26), channel_id=1, source_target_pairs={{0,8},{1,10},{2,9},{3,11},{4,12},{5,14},{6,13},{7,15},{8,0},{9,2},... | collective-permute-start | bytes 221192 | tf_op jit(solution)/shard_map/ppermute | solution.py:115
  30.5 7.1 %collective-permute-start.11 = (bf16[96,384]{1,0:T(8,128)(2,1)S(1)}, bf16[96,384]{1,0:T(8,128)(2,1)S(1)}, u32[]{:S(2)}, u32[]{:S(2)}) collective-permute-start(bf16[96,384]{1,0:T(8,128)(2,1)S(1)} %get-tuple-element.27), channel_id=1, source_target_pairs={{0,4},{1,6},{2,5},{3,7},{4,0},{5,2},{6,1},{7,3},{8,12},{9,14},{10,... | collective-permute-start | bytes 221192 | tf_op jit(solution)/shard_map/ppermute | solution.py:115
  30.7 7.0 %collective-permute-start.12 = (bf16[96,384]{1,0:T(8,128)(2,1)S(1)}, bf16[96,384]{1,0:T(8,128)(2,1)S(1)}, u32[]{:S(2)}, u32[]{:S(2)}) collective-permute-start(bf16[96,384]{1,0:T(8,128)(2,1)S(1)} %get-tuple-element.28), channel_id=1, source_target_pairs={{0,12},{1,14},{2,13},{3,15},{4,8},{5,10},{6,9},{7,11},{8,4},{9,6},... | collective-permute-start | bytes 221192 | tf_op jit(solution)/shard_map/ppermute | solution.py:115
  32.7 5.8 %collective-permute-start.13 = (bf16[96,384]{1,0:T(8,128)(2,1)S(1)}, bf16[96,384]{1,0:T(8,128)(2,1)S(1)}, u32[]{:S(2)}, u32[]{:S(2)}) collective-permute-start(bf16[96,384]{1,0:T(8,128)(2,1)S(1)} %get-tuple-element.25.kept), channel_id=1, source_target_pairs={{1,2},{2,1},{5,6},{6,5},{9,10},{10,9},{13,14},{14,13},{17,18},{18,... | collective-permute-start | bytes 221192 | tf_op jit(solution)/shard_map/ppermute | solution.py:115

commit v4 on v3

--- a/solution.py
+++ b/solution.py
@@ -389,12 +389,11 @@
     late = blocks - 1
     whole = [offset for offset in (far, *range(1, far), *range(far + 1, blocks)) if offset != late]
     split = [(late, piece) for piece in range(pieces)]
-    return (*[(offset, 0) for offset in whole], *split[:-1], (0, 0), split[-1])
+    return (*[(offset, 0) for offset in whole], (0, 0), *split)
 
 
 def return_order(blocks):
-    far = blocks // 2
-    return (*range(far, blocks), *reversed(range(far)))
+    return tuple(reversed(range(blocks)))
 
 
 def solution(mesh):

time: 39.4 us -> 39.4 us (level)
  no operation moved by 1% of the time
where the time goes in v4:
time: 39.4 us; the launch traced here: 39.1 us
  starting transfers between devices  24 us (61%)
  waiting for transfers between devices  9.16 us (23%)
  Pallas kernels  5.57 us (14%)
    ppermute x9, starting transfers between devices, swapped(): return lax.ppermute(array, MESH_TAIL, pairs)  23 us
    ppermute x9, waiting for transfers between devices, swapped(): return lax.ppermute(array, MESH_TAIL, pairs)  8.74 us
    pallas_call x2, Pallas kernels, pack(): pl.pallas_call(functools.partial(pack_kernel, tuple(heads), width), out_s...  2.61 us
    pallas_call x2, Pallas kernels, by_heads(): pl.pallas_call(functools.partial(attend_kernel, offsets, rows, tuple(rang...  2.03 us
    ppermute x5, starting transfers between devices, by_heads(): other[key] = lax.ppermute(own[key], 'head', [(0, 1), (1, 0)])  1.04 us
  transfers between devices with their start and end apart: 14, of which 6 were waited for; matrix products, arithmetic and copies ran while one was open for 1% of the time, Pallas kernels for 6%

profile of v4, /device:TPU:1, one launch (start us, length us, event | category | flops | bytes accessed | tf_op | source)
XLA Modules:
  0.0 39.1 jit_solution(3238291025150916209)
XLA Ops:
  0.0 1.5 %shard_map.74 = (bf16[240,384]{1,0:T(8,128)(2,1)S(1)}, bf16[256,384]{1,0:T(8,128)(2,1)S(1)}, bf16[240,256]{1,0:T(8,128)(2,1)S(1)}, bf16[240,128]{1,0:T(8,128)(2,1)S(1)}) custom-call(bf16[96,1536]{1,0:T(8,128)(2,1)} %bitcast.3, bf16[96,1536]{1,0:T(8,128)(2,1)} %bitcast.5, bf16[96,1536]{1,0:T(8,128)(2,1)} %hidden_hbm.3, f32[1,128]{1,0:T(1,128)} %qgain_hbm.3, ...), custom_call_target="tpu_custom_call" | custom-call | tf_op jit(solution)/shard_map/pallas_call | solution.py:324
  1.5 4.5 %collective-permute-start.2 = (bf16[256,384]{1,0:T(8,128)(2,1)S(1)}, bf16[256,384]{1,0:T(8,128)(2,1)S(1)}, u32[]{:S(2)}, u32[]{:S(2)}) collective-permute-start(bf16[256,384]{1,0:T(8,128)(2,1)S(1)} %get-tuple-element.18), channel_id=1, source_target_pairs={{0,0},{1,2},{2,1},{3,3},{4,4},{5,6},{6,5},{7,7},{8,8},{9,10},{10,9... | collective-permute-start | bytes 589832 | tf_op jit(solution)/shard_map/ppermute | solution.py:115
  6.0 1.1 %shard_map.73 = bf16[240,384]{1,0:T(8,128)(2,1)S(1)} custom-call(bf16[96,1536]{1,0:T(8,128)(2,1)} %bitcast.4, bf16[96,1536]{1,0:T(8,128)(2,1)} %bitcast.6, bf16[96,1536]{1,0:T(8,128)(2,1)} %hidden_hbm.3, f32[1,128]{1,0:T(1,128)} %qgain_hbm.3, f32[1,128]{1,0:T(1,128)} %kgain_hbm.3, f32[1,1536]{1,0:T(1,128)} %gate_hbm.3), custom_call_target="tpu_custom_call" | custom-call | tf_op jit(solution)/shard_map/pallas_call | solution.py:324
  7.1 2.1 %collective-permute-start = (bf16[240,384]{1,0:T(8,128)(2,1)S(1)}, bf16[240,384]{1,0:T(8,128)(2,1)S(1)}, u32[]{:S(2)}, u32[]{:S(2)}) collective-permute-start(bf16[240,384]{1,0:T(8,128)(2,1)S(1)} %shard_map.73), channel_id=1, source_target_pairs={{0,8},{1,10},{2,9},{3,11},{4,12},{5,14},{6,13},{7,15},{8,0},{9,2},... | collective-permute-start | bytes 552968 | tf_op jit(solution)/shard_map/ppermute | solution.py:115
  9.2 2.7 %collective-permute-start.1 = (bf16[240,384]{1,0:T(8,128)(2,1)S(1)}, bf16[240,384]{1,0:T(8,128)(2,1)S(1)}, u32[]{:S(2)}, u32[]{:S(2)}) collective-permute-start(bf16[240,384]{1,0:T(8,128)(2,1)S(1)} %get-tuple-element.17), channel_id=1, source_target_pairs={{0,4},{1,6},{2,5},{3,7},{4,0},{5,2},{6,1},{7,3},{8,12},{9,14},{10,... | collective-permute-start | bytes 552968 | tf_op jit(solution)/shard_map/ppermute | solution.py:115
  12.0 4.4 %collective-permute-start.3 = (bf16[240,128]{1,0:T(8,128)(2,1)S(1)}, bf16[240,128]{1,0:T(8,128)(2,1)S(1)}, u32[]{:S(2)}, u32[]{:S(2)}) collective-permute-start(bf16[240,128]{1,0:T(8,128)(2,1)S(1)} %get-tuple-element.19), channel_id=1, source_target_pairs={{0,12},{1,14},{2,13},{3,15},{4,8},{5,10},{6,9},{7,11},{8,4},{9,6},... | collective-permute-start | bytes 184328 | tf_op jit(solution)/shard_map/ppermute | solution.py:115
  16.4 4.4 %collective-permute-done.8.refs_4_ = bf16[240,256]{1,0:T(8,128)(2,1)S(1)} collective-permute-done((bf16[240,256]{1,0:T(8,128)(2,1)S(1)}, bf16[240,256]{1,0:T(8,128)(2,1)S(1)}, u32[]{:S(2)}, u32[]{:S(2)}) %collective-permute-start.8) | collective-permute-done | bytes 122912 | tf_op jit(solution)/shard_map/ppermute | solution.py:115
  20.9 1.0 %collective-permute-done.refs_1_ = bf16[240,384]{1,0:T(8,128)(2,1)S(1)} collective-permute-done((bf16[240,384]{1,0:T(8,128)(2,1)S(1)}, bf16[240,384]{1,0:T(8,128)(2,1)S(1)}, u32[]{:S(2)}, u32[]{:S(2)}) %collective-permute-start) | collective-permute-done | bytes 184352 | tf_op jit(solution)/shard_map/ppermute | solution.py:115
  21.9 0.5 %collective-permute-start.5 = (bf16[240,384]{1,0:T(8,128)(2,1)S(1)}, bf16[240,384]{1,0:T(8,128)(2,1)S(1)}, u32[]{:S(2)}, u32[]{:S(2)}) collective-permute-start(bf16[240,384]{1,0:T(8,128)(2,1)S(1)} %collective-permute-done.1.refs_2_), channel_id=1, source_target_pairs={{0,1},{1,0},{2,3},{3,2},{4,5},{5,4},{6,7},{7,6},{8,9},{9,8},{10,11... | collective-permute-start | bytes 552968 | tf_op jit(solution)/shard_map/ppermute | solution.py:342
  22.5 0.1 fusion
  22.6 0.5 %collective-permute-start.7 = (bf16[240,128]{1,0:T(8,128)(2,1)S(1)}, bf16[240,128]{1,0:T(8,128)(2,1)S(1)}, u32[]{:S(2)}, u32[]{:S(2)}) collective-permute-start(bf16[240,128]{1,0:T(8,128)(2,1)S(1)} %collective-permute-done.3.refs_4_), channel_id=1, source_target_pairs={{0,1},{1,0},{2,3},{3,2},{4,5},{5,4},{6,7},{7,6},{8,9},{9,8},{10,11... | collective-permute-start | bytes 184328 | tf_op jit(solution)/shard_map/ppermute | solution.py:342
  23.1 0.1 reshape.8.query_ids
  23.2 0.2 mask.1.refs_0_
  23.4 0.1 collective-permute-done.5.refs_6_
  23.6 0.3 collective-permute-done.6.refs_7_
  23.9 1.1 %shard_map.75 = (bf16[96,384]{1,0:T(8,128)(2,1)S(1)}, bf16[96,384]{1,0:T(8,128)(2,1)S(1)}, bf16[96,384]{1,0:T(8,128)(2,1)S(1)}, bf16[96,384]{1,0:T(8,128)(2,1)S(1)}) custom-call(f32[384,384]{1,0:T(8,128)S(1)} %mask.1.refs_0_, bf16[240,384]{1,0:T(8,128)(2,1)S(1)} %collective-permute-done.refs_1_, bf16[240,384]{1,0:T(8,128)(2,1)S(1)} %collective-permute-done.1.refs_2_, ...), custom_call_target="tpu_custom_call" | custom-call | tf_op jit(solution)/shard_map/pallas_call | solution.py:361
  25.0 0.9 %shard_map.76 = (bf16[96,384]{1,0:T(8,128)(2,1)S(1)}, bf16[96,384]{1,0:T(8,128)(2,1)S(1)}, bf16[96,384]{1,0:T(8,128)(2,1)S(1)}, bf16[96,384]{1,0:T(8,128)(2,1)S(1)}) custom-call(f32[384,384]{1,0:T(8,128)S(1)} %mask.1.refs_0_, ...), custom_call_target="tpu_custom_call", output_to_operand_aliasing={{0}: (9, {}), {1}: (10, {}), {2}: (11, {}), {3}: (12, {})} | custom-call | tf_op jit(solution)/shard_map/pallas_call | solution.py:361
  25.9 4.6 %collective-permute-start.10 = (bf16[96,384]{1,0:T(8,128)(2,1)S(1)}, bf16[96,384]{1,0:T(8,128)(2,1)S(1)}, u32[]{:S(2)}, u32[]{:S(2)}) collective-permute-start(bf16[96,384]{1,0:T(8,128)(2,1)S(1)} %get-tuple-element.26), channel_id=1, source_target_pairs={{0,8},{1,10},{2,9},{3,11},{4,12},{5,14},{6,13},{7,15},{8,0},{9,2},... | collective-permute-start | bytes 221192 | tf_op jit(solution)/shard_map/ppermute | solution.py:115
  30.5 0.2 collective-permute-start.11
  30.7 2.0 %collective-permute-start.13 = (bf16[96,384]{1,0:T(8,128)(2,1)S(1)}, bf16[96,384]{1,0:T(8,128)(2,1)S(1)}, u32[]{:S(2)}, u32[]{:S(2)}) collective-permute-start(bf16[96,384]{1,0:T(8,128)(2,1)S(1)} %get-tuple-element.28), channel_id=1, source_target_pairs={{0,12},{1,14},{2,13},{3,15},{4,8},{5,10},{6,9},{7,11},{8,4},{9,6},... | collective-permute-start | bytes 221192 | tf_op jit(solution)/shard_map/ppermute | solution.py:115
  32.7 2.5 %collective-permute-start.12 = (bf16[96,384]{1,0:T(8,128)(2,1)S(1)}, bf16[96,384]{1,0:T(8,128)(2,1)S(1)}, u32[]{:S(2)}, u32[]{:S(2)}) collective-permute-start(bf16[96,384]{1,0:T(8,128)(2,1)S(1)} %get-tuple-element.25.kept), channel_id=1, source_target_pairs={{1,2},{2,1},{5,6},{6,5},{9,10},{10,9},{13,14},{14,13},{17,18},{18,... | collective-permute-start | bytes 221192 | tf_op jit(solution)/shard_map/ppermute | solution.py:115
  35.1 2.5 %collective-permute-done.11.refs_1_ = bf16[96,384]{1,0:T(8,128)(2,1)S(1)} collective-permute-done((bf16[96,384]{1,0:T(8,128)(2,1)S(1)}, bf16[96,384]{1,0:T(8,128)(2,1)S(1)}, u32[]{:S(2)}, u32[]{:S(2)}) %collective-permute-start.11) | collective-permute-done | bytes 73760 | tf_op jit(solution)/shard_map/ppermute | solution.py:115
  37.6 0.8 %collective-permute-done.12.refs_2_ = bf16[96,384]{1,0:T(8,128)(2,1)S(1)} collective-permute-done((bf16[96,384]{1,0:T(8,128)(2,1)S(1)}, bf16[96,384]{1,0:T(8,128)(2,1)S(1)}, u32[]{:S(2)}, u32[]{:S(2)}) %collective-permute-start.12) | collective-permute-done | bytes 73760 | tf_op jit(solution)/shard_map/ppermute | solution.py:115
  38.4 0.7 %join.1 = bf16[96,1536]{1,0:T(8,128)(2,1)} custom-call(bf16[96,384]{1,0:T(8,128)(2,1)S(1)} %get-tuple-element.25.kept, bf16[96,384]{1,0:T(8,128)(2,1)S(1)} %collective-permute-done.10.refs_0_, bf16[96,384]{1,0:T(8,128)(2,1)S(1)} %collective-permute-done.11.refs_1_, bf16[96,384]{1,0:T(8,128)(2,1)S(1)} %collective-permute-done.12.refs_2_, ...), custom_call_target="tpu_custom_call" | custom-call | tf_op jit(solution)/shard_map/join/pallas_call | solution.py:375
  (16 shorter events, 0.2 us)
Async XLA Ops:
  1.5 20.9 %collective-permute-start.2 = (bf16[256,384]{1,0:T(8,128)(2,1)S(1)}, bf16[256,384]{1,0:T(8,128)(2,1)S(1)}, u32[]{:S(2)}, u32[]{:S(2)}) collective-permute-start(bf16[256,384]{1,0:T(8,128)(2,1)S(1)} %get-tuple-element.18), channel_id=1, source_target_pairs={{0,0},{1,2},{2,1},{3,3},{4,4},{5,6},{6,5},{7,7},{8,8},{9,10},{10,9... | collective-permute-start | bytes 589832 | tf_op jit(solution)/shard_map/ppermute | solution.py:115
  7.1 14.8 %collective-permute-start = (bf16[240,384]{1,0:T(8,128)(2,1)S(1)}, bf16[240,384]{1,0:T(8,128)(2,1)S(1)}, u32[]{:S(2)}, u32[]{:S(2)}) collective-permute-start(bf16[240,384]{1,0:T(8,128)(2,1)S(1)} %shard_map.73), channel_id=1, source_target_pairs={{0,8},{1,10},{2,9},{3,11},{4,12},{5,14},{6,13},{7,15},{8,0},{9,2},... | collective-permute-start | bytes 552968 | tf_op jit(solution)/shard_map/ppermute | solution.py:115
  9.2 12.7 %collective-permute-start.1 = (bf16[240,384]{1,0:T(8,128)(2,1)S(1)}, bf16[240,384]{1,0:T(8,128)(2,1)S(1)}, u32[]{:S(2)}, u32[]{:S(2)}) collective-permute-start(bf16[240,384]{1,0:T(8,128)(2,1)S(1)} %get-tuple-element.17), channel_id=1, source_target_pairs={{0,4},{1,6},{2,5},{3,7},{4,0},{5,2},{6,1},{7,3},{8,12},{9,14},{10,... | collective-permute-start | bytes 552968 | tf_op jit(solution)/shard_map/ppermute | solution.py:115
  12.0 8.9 %collective-permute-start.8 = (bf16[240,256]{1,0:T(8,128)(2,1)S(1)}, bf16[240,256]{1,0:T(8,128)(2,1)S(1)}, u32[]{:S(2)}, u32[]{:S(2)}) collective-permute-start(bf16[240,256]{1,0:T(8,128)(2,1)S(1)} %get-tuple-element.20), channel_id=1, source_target_pairs={{0,12},{1,14},{2,13},{3,15},{4,8},{5,10},{6,9},{7,11},{8,4},{9,6},... | collective-permute-start | bytes 368648 | tf_op jit(solution)/shard_map/ppermute | solution.py:115
  12.0 10.6 %collective-permute-start.3 = (bf16[240,128]{1,0:T(8,128)(2,1)S(1)}, bf16[240,128]{1,0:T(8,128)(2,1)S(1)}, u32[]{:S(2)}, u32[]{:S(2)}) collective-permute-start(bf16[240,128]{1,0:T(8,128)(2,1)S(1)} %get-tuple-element.19), channel_id=1, source_target_pairs={{0,12},{1,14},{2,13},{3,15},{4,8},{5,10},{6,9},{7,11},{8,4},{9,6},... | collective-permute-start | bytes 184328 | tf_op jit(solution)/shard_map/ppermute | solution.py:115
  16.4 6.1 %copy-start = (s32[384]{0:T(512)S(1)}, s32[384]{0:T(512)}, u32[]{:S(2)}) copy-start(s32[384]{0:T(512)} %param.13) | copy-start | bytes 4612
  20.9 2.6 %collective-permute-start.9 = (bf16[240,256]{1,0:T(8,128)(2,1)S(1)}, bf16[240,256]{1,0:T(8,128)(2,1)S(1)}, u32[]{:S(2)}, u32[]{:S(2)}) collective-permute-start(bf16[240,256]{1,0:T(8,128)(2,1)S(1)} %collective-permute-done.8.refs_4_), channel_id=1, source_target_pairs={{0,1},{1,0},{2,3},{3,2},{4,5},{5,4},{6,7},{7,6},{8,9},{9,8},{10,11... | collective-permute-start | bytes 368648 | tf_op jit(solution)/shard_map/ppermute | solution.py:342
  21.9 1.5 %collective-permute-start.4 = (bf16[240,384]{1,0:T(8,128)(2,1)S(1)}, bf16[240,384]{1,0:T(8,128)(2,1)S(1)}, u32[]{:S(2)}, u32[]{:S(2)}) collective-permute-start(bf16[240,384]{1,0:T(8,128)(2,1)S(1)} %collective-permute-done.refs_1_), channel_id=1, source_target_pairs={{0,1},{1,0},{2,3},{3,2},{4,5},{5,4},{6,7},{7,6},{8,9},{9,8},{10,11... | collective-permute-start | bytes 552968 | tf_op jit(solution)/shard_map/ppermute | solution.py:342
  21.9 1.7 %collective-permute-start.5 = (bf16[240,384]{1,0:T(8,128)(2,1)S(1)}, bf16[240,384]{1,0:T(8,128)(2,1)S(1)}, u32[]{:S(2)}, u32[]{:S(2)}) collective-permute-start(bf16[240,384]{1,0:T(8,128)(2,1)S(1)} %collective-permute-done.1.refs_2_), channel_id=1, source_target_pairs={{0,1},{1,0},{2,3},{3,2},{4,5},{5,4},{6,7},{7,6},{8,9},{9,8},{10,11... | collective-permute-start | bytes 552968 | tf_op jit(solution)/shard_map/ppermute | solution.py:342
  22.4 1.5 %collective-permute-start.6 = (bf16[256,384]{1,0:T(8,128)(2,1)S(1)}, bf16[256,384]{1,0:T(8,128)(2,1)S(1)}, u32[]{:S(2)}, u32[]{:S(2)}) collective-permute-start(bf16[256,384]{1,0:T(8,128)(2,1)S(1)} %collective-permute-done.2.refs_3_), channel_id=1, source_target_pairs={{0,1},{1,0},{2,3},{3,2},{4,5},{5,4},{6,7},{7,6},{8,9},{9,8},{10,11... | collective-permute-start | bytes 589832 | tf_op jit(solution)/shard_map/ppermute | solution.py:342
  22.6 2.4 %collective-permute-start.7 = (bf16[240,128]{1,0:T(8,128)(2,1)S(1)}, bf16[240,128]{1,0:T(8,128)(2,1)S(1)}, u32[]{:S(2)}, u32[]{:S(2)}) collective-permute-start(bf16[240,128]{1,0:T(8,128)(2,1)S(1)} %collective-permute-done.3.refs_4_), channel_id=1, source_target_pairs={{0,1},{1,0},{2,3},{3,2},{4,5},{5,4},{6,7},{7,6},{8,9},{9,8},{10,11... | collective-permute-start | bytes 184328 | tf_op jit(solution)/shard_map/ppermute | solution.py:342
  25.9 9.2 %collective-permute-start.10 = (bf16[96,384]{1,0:T(8,128)(2,1)S(1)}, bf16[96,384]{1,0:T(8,128)(2,1)S(1)}, u32[]{:S(2)}, u32[]{:S(2)}) collective-permute-start(bf16[96,384]{1,0:T(8,128)(2,1)S(1)} %get-tuple-element.26), channel_id=1, source_target_pairs={{0,8},{1,10},{2,9},{3,11},{4,12},{5,14},{6,13},{7,15},{8,0},{9,2},... | collective-permute-start | bytes 221192 | tf_op jit(solution)/shard_map/ppermute | solution.py:115
  30.5 7.1 %collective-permute-start.11 = (bf16[96,384]{1,0:T(8,128)(2,1)S(1)}, bf16[96,384]{1,0:T(8,128)(2,1)S(1)}, u32[]{:S(2)}, u32[]{:S(2)}) collective-permute-start(bf16[96,384]{1,0:T(8,128)(2,1)S(1)} %get-tuple-element.27), channel_id=1, source_target_pairs={{0,4},{1,6},{2,5},{3,7},{4,0},{5,2},{6,1},{7,3},{8,12},{9,14},{10,... | collective-permute-start | bytes 221192 | tf_op jit(solution)/shard_map/ppermute | solution.py:115
  30.7 7.0 %collective-permute-start.13 = (bf16[96,384]{1,0:T(8,128)(2,1)S(1)}, bf16[96,384]{1,0:T(8,128)(2,1)S(1)}, u32[]{:S(2)}, u32[]{:S(2)}) collective-permute-start(bf16[96,384]{1,0:T(8,128)(2,1)S(1)} %get-tuple-element.28), channel_id=1, source_target_pairs={{0,12},{1,14},{2,13},{3,15},{4,8},{5,10},{6,9},{7,11},{8,4},{9,6},... | collective-permute-start | bytes 221192 | tf_op jit(solution)/shard_map/ppermute | solution.py:115
  32.7 5.7 %collective-permute-start.12 = (bf16[96,384]{1,0:T(8,128)(2,1)S(1)}, bf16[96,384]{1,0:T(8,128)(2,1)S(1)}, u32[]{:S(2)}, u32[]{:S(2)}) collective-permute-start(bf16[96,384]{1,0:T(8,128)(2,1)S(1)} %get-tuple-element.25.kept), channel_id=1, source_target_pairs={{1,2},{2,1},{5,6},{6,5},{9,10},{10,9},{13,14},{14,13},{17,18},{18,... | collective-permute-start | bytes 221192 | tf_op jit(solution)/shard_map/ppermute | solution.py:115
